TPU v7x, 256 devices: a whole 4x4x8 slice. The times are simulated.
256 devices in a mesh: slab: 32 (over x, z), col: 8 (over y, core).
Axes of the slice: x: 4, y: 4, z: 8, core: 2. Of those that a mesh axis runs over, the one named last changes fastest.
Arguments:
- order_params: float32 [16, 256, 64, 256], P(None, 'slab', 'col'), may hold values from 0 to 0.5
- layer_mask: int32 [256, 64, 256], P('slab', 'col'), may hold values 0 or 1
- coarse_temp: float32 [192, 32, 128], P('slab', 'col'), may hold values from 0.5 to 1.5, as said below
- coarse_rows: int32 [32], replicated, may hold values from 2 to 6, as said below
- grain_ids: int32 [32, 8, 16], replicated, may hold values from 0 to 2207, as said below
- energy: float32 [2208], replicated, may hold values from 0.5 to 6
Outputs:
- evolved: float32 [16, 256, 64, 256], P(None, 'slab', 'col')
Inputs may be any that keep to these rules, and one draw needn't show every extreme that they name: coarse_rows sums to 128; the s-th block of coarse planes begins within 1 planes of s * 4; some entry equals 6. `coarse_temp`: rows of one index of slab past its entry of coarse_rows are not part of the field. `grain_ids`: the 16 ids of a block are distinct; a block shares exactly 4 ids with each block beside it along slab and along col and none with any other block.
All inputs are finite; a program needn't handle non-finite values. No bound on the sum of `layer_mask` on one device may be relied on, other than what follows from the above.
Results may differ from a plain program's by a relative error of at most 0.0001.
Values sent between devices are 32-bit elements; how exact they have to be, the bound alone decides.
A program may use at most 64 MiB of HBM per device.

v0:
```python
import jax
import jax.numpy as jnp
from jax import lax
from jax.sharding import Mesh
from jax.sharding import PartitionSpec as P

STEPS = 4
SLAB = ("slab_0", "slab_1")
COL = ("col_0", "col_1")


FULL_ACCURACY = lax.Precision.HIGHEST
TIME_STEP = 0.05
COUPLING = 1.5


def sent_to_all(array, axis):
    copies = jnp.broadcast_to(array, (lax.axis_size(axis), *array.shape))
    return lax.all_to_all(copies, axis, split_axis=0, concat_axis=0, tiled=True)


def taken_together(array, axis):
    everything = sent_to_all(array, axis)
    return jnp.sum(everything, axis=0)


def one_axis_at_a_time(array, axes):
    far, near = axes
    nearer = taken_together(array, near)
    return taken_together(nearer, far)


def padded_2(cells, sides, width):
    for axis, dim in sides:
        count = lax.axis_size(axis)
        ends = count - 1
        head = lax.slice_in_dim(cells, 0, width, axis=dim)
        tail = lax.slice_in_dim(cells, cells.shape[dim] - width, cells.shape[dim], axis=dim)
        cells = jnp.concatenate(
            [
                lax.ppermute(tail, axis, [(i, (i + 1) % count) for i in range(ends)]),
                cells,
                lax.ppermute(head, axis, [((i + 1) % count, i) for i in range(ends)]),
            ],
            axis=dim,
        )
    return cells


def with_halo(array, sides, width):
    edges = {}
    for axis, dim in sides:
        peers, length = (lax.axis_size(axis), array.shape[dim])
        up = [(i, (i + 1) % peers) for i in range(peers - 1)]
        last = lax.slice_in_dim(array, length - width, length, axis=dim)
        first = lax.slice_in_dim(array, 0, width, axis=dim)
        edges[dim] = (
            lax.ppermute(last, axis, up),
            lax.ppermute(first, axis, [(b, a) for a, b in up]),
        )
    done = []
    for _, dim in sides:
        low, high = edges[dim]
        around = [(width, width) if d in done else (0, 0) for d in range(array.ndim)]
        array = jnp.concatenate([jnp.pad(low, around), array, jnp.pad(high, around)], axis=dim)
        done.append(dim)
    return array


def packed_total(arrays, axis):
    line, at, done = (jnp.concatenate([a.reshape(-1) for a in arrays]), 0, [])
    so_far = one_axis_at_a_time(line, axis)
    for a in arrays:
        done.append(so_far[at : at + a.size].reshape(a.shape))
        at += a.size
    return tuple(done)


def node_weights(fine_index, coarse_count):
    lower_index = (2 * fine_index - 1) // 4
    weight = (2 * fine_index - 1 - 4 * lower_index).astype(jnp.float32) / 4.0
    lower_node = jnp.clip(lower_index, 0, coarse_count - 1)
    upper_node = jnp.clip(lower_index + 1, 0, coarse_count - 1)
    return (lower_node, upper_node, weight)


def interpolation_matrix(lower_node, upper_node, weight, column_count):
    columns = jnp.arange(column_count, dtype=jnp.int32)
    lower_hit = (columns[None, :] == lower_node[:, None]).astype(jnp.float32)
    upper_hit = (columns[None, :] == upper_node[:, None]).astype(jnp.float32)
    return (1.0 - weight)[:, None] * lower_hit + weight[:, None] * upper_hit


def pick_entry(values, slab_iota, position):
    return jnp.sum(jnp.where(slab_iota == position, values, 0))


def block_ids(grain_ids, slab_pos, col_pos):
    slab_row = lax.dynamic_index_in_dim(grain_ids, slab_pos, 0, keepdims=False)
    return lax.dynamic_index_in_dim(slab_row, col_pos, 0, keepdims=False)


def slot_match(mine, theirs):
    return (mine[:, None] == theirs[None, :]).astype(jnp.float32)


def apply_slots(matrix, face_cells):
    return jnp.einsum("qr,ryz->qyz", matrix, face_cells, precision=FULL_ACCURACY)


def rates(fields, laplace, grain_mobility, slot_energy):
    squares = jnp.sum(fields * fields, axis=0)
    force = (
        -fields
        + fields * fields * fields
        + 2.0 * COUPLING * fields * (squares - fields * fields)
        - laplace
        - slot_energy * fields * (1.0 - fields)
    )
    return -grain_mobility * force


def total_rate(local_rate):
    return one_axis_at_a_time(local_rate, (("slab_0", "slab_1"), ("col_0", "col_1")))


def per_device(order_params, layer_mask, coarse_temp, coarse_rows, grain_ids, energy):
    slot_count, cells_x, cells_y, cells_z = order_params.shape
    slab_count = lax.axis_size(SLAB)
    col_count = lax.axis_size(COL)
    slab_at = lax.axis_index(SLAB)
    col_at = lax.axis_index(COL)
    capacity = coarse_temp.shape[0]
    coarse_y = coarse_temp.shape[1]
    coarse_z = coarse_temp.shape[2]
    extended = padded_2(coarse_temp, ((COL, 1),), 1)
    block_ends = jnp.cumsum(coarse_rows)
    block_starts = block_ends - coarse_rows
    slab_iota = jnp.arange(slab_count, dtype=jnp.int32)
    start_own = pick_entry(block_starts, slab_iota, slab_at)
    end_own = pick_entry(block_ends, slab_iota, slab_at)
    start_prev = pick_entry(block_starts, slab_iota, slab_at - 1)
    fine_x = slab_at * cells_x + jnp.arange(cells_x, dtype=jnp.int32)
    lower_x, upper_x, weight_x = node_weights(fine_x, slab_count * (cells_x // 2))
    source = padded_2(extended, ((SLAB, 0),), capacity)

    def locate(plane):
        return jnp.where(
            plane < start_own,
            plane - start_prev,
            jnp.where(
                plane < end_own, capacity + plane - start_own, 2 * capacity + plane - end_own
            ),
        )

    along_x = interpolation_matrix(locate(lower_x), locate(upper_x), weight_x, source.shape[0])
    coarse_slab = jnp.einsum("ir,ryz->iyz", along_x, source, precision=FULL_ACCURACY)
    fine_y = col_at * cells_y + jnp.arange(cells_y, dtype=jnp.int32)
    lower_y, upper_y, weight_y = node_weights(fine_y, col_count * coarse_y)
    y_offset = col_at * coarse_y - 1
    along_y = interpolation_matrix(lower_y - y_offset, upper_y - y_offset, weight_y, coarse_y + 2)
    coarse_columns = jnp.einsum("jy,iyz->ijz", along_y, coarse_slab, precision=FULL_ACCURACY)
    lower_z, upper_z, weight_z = node_weights(jnp.arange(cells_z, dtype=jnp.int32), coarse_z)
    vertical_direction = interpolation_matrix(lower_z, upper_z, weight_z, coarse_z)
    thermal_profile = jnp.einsum(
        "au,hwu->hwa", vertical_direction, coarse_columns, precision=FULL_ACCURACY
    )
    grain_mobility = jnp.exp(2.0 * (thermal_profile - 1.0))
    deposited = layer_mask.astype(jnp.float32)
    local_mobility = jnp.sum(deposited * grain_mobility)
    mobility_sum = jnp.float32(1.0)
    own_ids = block_ids(grain_ids, slab_at, col_at)
    prev_slab_ids = block_ids(grain_ids, jnp.maximum(slab_at - 1, 0), col_at)
    next_slab_ids = block_ids(grain_ids, jnp.minimum(slab_at + 1, slab_count - 1), col_at)
    prev_col_ids = block_ids(grain_ids, slab_at, jnp.maximum(col_at - 1, 0))
    next_col_ids = block_ids(grain_ids, slab_at, jnp.minimum(col_at + 1, col_count - 1))
    grain_iota = jnp.arange(energy.shape[0], dtype=jnp.int32)
    slot_energy = jnp.sum(
        jnp.where(own_ids[:, None] == grain_iota[None, :], energy[None, :], 0.0), axis=1
    )[:, None, None, None]
    below_map = slot_match(own_ids, prev_slab_ids)
    above_map = slot_match(own_ids, next_slab_ids)
    left_map = slot_match(own_ids, prev_col_ids)
    right_map = slot_match(own_ids, next_col_ids)
    fields = order_params
    zero_plane = jnp.zeros((slot_count, cells_x, cells_y, 1), jnp.float32)
    for step_index in range(STEPS):
        padded = with_halo(fields, ((SLAB, 1), (COL, 2)), 1)
        below = apply_slots(below_map, padded[:, 0, 1:-1])
        above = apply_slots(above_map, padded[:, -1, 1:-1])
        left_side = apply_slots(left_map, padded[:, 1:-1, 0])
        right_side = apply_slots(right_map, padded[:, 1:-1, -1])
        x_low = jnp.concatenate([below[:, None], fields[:, :-1]], axis=1)
        x_high = jnp.concatenate([fields[:, 1:], above[:, None]], axis=1)
        y_low = jnp.concatenate([left_side[:, :, None], fields[:, :, :-1]], axis=2)
        y_high = jnp.concatenate([fields[:, :, 1:], right_side[:, :, None]], axis=2)
        z_low = jnp.concatenate([zero_plane, fields[..., :-1]], axis=3)
        z_high = jnp.concatenate([fields[..., 1:], zero_plane], axis=3)
        laplace = x_low + x_high + y_low + y_high + z_low + z_high - 6.0 * fields
        rate = rates(fields, laplace, grain_mobility, slot_energy)
        local_rate = jnp.sum(deposited * jnp.sum(rate, axis=0))
        if step_index == 0:
            rate_sum, mobility_whole = packed_total(
                (local_rate, local_mobility), (("slab_0", "slab_1"), ("col_0", "col_1"))
            )
            mobility_sum = mobility_whole * slot_count
        else:
            rate_sum = total_rate(local_rate)
        multiplier = rate_sum / mobility_sum
        fields = fields + TIME_STEP * deposited * (rate - grain_mobility * multiplier)
    return fields


def solution(mesh):
    split = Mesh(mesh.devices.reshape(4, 8, 4, 2), ("slab_0", "slab_1", "col_0", "col_1"))
    placed = (P(None, SLAB, COL, None), P(SLAB, COL, None), P(SLAB, COL, None), P(), P(), P())
    return jax.shard_map(
        per_device, mesh=split, in_specs=placed, out_specs=P(None, SLAB, COL, None), check_vma=False
    )
```

profile of v0, /device:TPU:1, one launch (start us, length us, event | category | flops | bytes accessed | tf_op | source)
XLA Modules:
  0.0 214.0 jit_solution(15419007011993054298)
XLA Ops:
  0.0 0.8 fusion.240
  0.8 4.6 %collective-permute-start = (f32[6,1,128]{2,0,1:T(8,128)S(1)}, f32[6,1,128]{2,0,1:T(8,128)S(1)}, u32[]{:S(2)}, u32[]{:S(2)}) collective-permute-start(f32[6,1,128]{2,0,1:T(8,128)S(1)} %copy.144), channel_id=1, source_target_pairs={{0,1},{1,2},{2,3},{3,4},{4,5},{5,6},{6,7},{8,9},{9,10},{10,11},{11... | collective-permute-start | bytes 9224 | tf_op jit(solution)/shard_map/ppermute | solution.py:41
  5.4 1.9 collective-permute-start.1
  7.4 1.0 fusion.239
  8.4 4.2 %collective-permute-start.4 = (f32[16,1,8,256]{3,0,2,1:T(8,128)S(1)}, f32[16,1,8,256]{3,0,2,1:T(8,128)}, u32[]{:S(2)}, u32[]{:S(2)}) collective-permute-start(f32[16,1,8,256]{3,0,2,1:T(8,128)S(1)} %copy.137), channel_id=1, source_target_pairs={{0,8},{8,16},{16,24},{24,32},{32,40},{40,48},{48,56},{56,64},{64,7... | collective-permute-start | bytes 393224 | tf_op jit(solution)/shard_map/ppermute | solution.py:58
  13.3 1.3 collective-permute-start.5
  15.4 3.9 %collective-permute-start.6 = (f32[16,8,1,256]{3,0,1,2:T(8,128)}, f32[16,8,1,256]{3,0,1,2:T(8,128)}, u32[]{:S(2)}, u32[]{:S(2)}) collective-permute-start(f32[16,8,1,256]{3,0,1,2:T(8,128)} %copy.123), channel_id=1, source_target_pairs={{0,1},{1,2},{2,3},{3,4},{4,5},{5,6},{6,7},{8,9},{9,10},{10,11},{11... | collective-permute-start | bytes 393224 | tf_op jit(solution)/shard_map/ppermute | solution.py:58
  21.1 1.4 fusion.238
  22.5 1.5 fusion.236
  26.6 1.3 collective-permute-start.3
  27.9 4.9 %collective-permute-start.2 = (f32[6,6,128]{2,0,1:T(8,128)S(1)}, f32[6,6,128]{2,0,1:T(8,128)S(1)}, u32[]{:S(2)}, u32[]{:S(2)}) collective-permute-start(f32[6,6,128]{2,0,1:T(8,128)S(1)} %constant_dynamic-update-slice_fusion), channel_id=1, source_target_pairs={{0,8},{8,16},{16,24},{24,32},{32,40},{40,48},{48,56},{56,64},{64,7... | collective-permute-start | bytes 55304 | tf_op jit(solution)/shard_map/ppermute | solution.py:41
  32.8 1.8 compare_select_fusion.1
  34.7 1.5 copy.139
  36.6 0.9 copy-done.2
  39.8 1.9 collective-permute-start.7
  44.6 1.2 convolution_bitcast_fusion.15
  45.8 1.2 convolution_bitcast_fusion.14
  47.0 1.2 convolution_bitcast_fusion.13
  48.5 1.5 fusion.243
  50.7 1.3 pad_maximum_fusion
  52.0 9.4 %all_to_all.48 = f32[8,1,2]{2,1,0:T(1,128)S(1)} all-to-all(f32[8,1,2]{2,1,0:T(1,128)S(1)} %broadcast_in_dim.73), channel_id=1, replica_groups=mesh['slab_0'=4,'slab_1'=8,'col_0'=4,'col_1'=2] {'col_0','col_1'}, dimensions={0} | all-to-all | bytes 128 | tf_op jit(solution)/shard_map/all_to_all | solution.py:19
  61.5 19.9 %all_to_all.49 = f32[32,1,2]{2,1,0:T(1,128)S(1)} all-to-all(f32[32,1,2]{2,1,0:T(1,128)S(1)} %broadcast_in_dim.74), channel_id=1, replica_groups=mesh['slab_0'=4,'slab_1'=8,'col_0'=4,'col_1'=2] {'slab_0','slab_1'}, dimensions={0} | all-to-all | bytes 512 | tf_op jit(solution)/shard_map/all_to_all | solution.py:19
  83.2 0.7 multiply_add_fusion.3
  84.9 1.3 collective-permute-start.9
  86.2 4.0 %collective-permute-start.8 = (f32[16,1,8,256]{3,0,2,1:T(8,128)S(1)}, f32[16,1,8,256]{3,0,2,1:T(8,128)S(1)}, u32[]{:S(2)}, u32[]{:S(2)}) collective-permute-start(f32[16,1,8,256]{3,0,2,1:T(8,128)S(1)} %get-tuple-element.44), channel_id=1, source_target_pairs={{0,8},{8,16},{16,24},{24,32},{32,40},{40,48},{48,56},{56,64},{64,7... | collective-permute-start | bytes 393224 | tf_op jit(solution)/shard_map/ppermute | solution.py:58
  90.2 4.6 %collective-permute-start.11 = (f32[16,8,1,256]{3,0,2,1:T(8,128)S(1)}, f32[16,8,1,256]{3,0,2,1:T(8,128)S(1)}, u32[]{:S(2)}, u32[]{:S(2)}) collective-permute-start(f32[16,8,1,256]{3,0,2,1:T(8,128)S(1)} %get-tuple-element.39), channel_id=1, source_target_pairs={{1,0},{2,1},{3,2},{4,3},{5,4},{6,5},{7,6},{9,8},{10,9},{11,10},{12... | collective-permute-start | bytes 393224 | tf_op jit(solution)/shard_map/ppermute | solution.py:59
  94.8 2.1 collective-permute-start.10
  97.9 0.9 collective-permute-done.10
  99.1 1.1 fusion.244
  101.5 9.1 %all_to_all.50 = f32[8,1,1]{2,1,0:T(1,128)S(1)} all-to-all(f32[8,1,1]{2,1,0:T(1,128)S(1)} %broadcast_in_dim.79), channel_id=1, replica_groups=mesh['slab_0'=4,'slab_1'=8,'col_0'=4,'col_1'=2] {'col_0','col_1'}, dimensions={0} | all-to-all | bytes 64 | tf_op jit(solution)/shard_map/all_to_all | solution.py:19
  111.9 13.4 %all_to_all.51 = f32[32,1,1]{2,1,0:T(1,128)S(1)} all-to-all(f32[32,1,1]{2,1,0:T(1,128)S(1)} %broadcast_in_dim.80), channel_id=1, replica_groups=mesh['slab_0'=4,'slab_1'=8,'col_0'=4,'col_1'=2] {'slab_0','slab_1'}, dimensions={0} | all-to-all | bytes 256 | tf_op jit(solution)/shard_map/all_to_all | solution.py:19
  127.8 1.3 collective-permute-start.13
  129.1 4.0 %collective-permute-start.12 = (f32[16,1,8,256]{3,0,2,1:T(8,128)S(1)}, f32[16,1,8,256]{3,0,2,1:T(8,128)S(1)}, u32[]{:S(2)}, u32[]{:S(2)}) collective-permute-start(f32[16,1,8,256]{3,0,2,1:T(8,128)S(1)} %get-tuple-element.34), channel_id=1, source_target_pairs={{0,8},{8,16},{16,24},{24,32},{32,40},{40,48},{48,56},{56,64},{64,7... | collective-permute-start | bytes 393224 | tf_op jit(solution)/shard_map/ppermute | solution.py:58
  133.1 4.6 %collective-permute-start.15 = (f32[16,8,1,256]{3,0,2,1:T(8,128)S(1)}, f32[16,8,1,256]{3,0,2,1:T(8,128)S(1)}, u32[]{:S(2)}, u32[]{:S(2)}) collective-permute-start(f32[16,8,1,256]{3,0,2,1:T(8,128)S(1)} %get-tuple-element.29), channel_id=1, source_target_pairs={{1,0},{2,1},{3,2},{4,3},{5,4},{6,5},{7,6},{9,8},{10,9},{11,10},{12... | collective-permute-start | bytes 393224 | tf_op jit(solution)/shard_map/ppermute | solution.py:59
  137.7 2.1 collective-permute-start.14
  140.8 1.0 collective-permute-done.14
  142.0 1.1 fusion.245
  144.4 9.1 %all_to_all.52 = f32[8,1,1]{2,1,0:T(1,128)S(1)} all-to-all(f32[8,1,1]{2,1,0:T(1,128)S(1)} %broadcast_in_dim.156), channel_id=1, replica_groups=mesh['slab_0'=4,'slab_1'=8,'col_0'=4,'col_1'=2] {'col_0','col_1'}, dimensions={0} | all-to-all | bytes 64 | tf_op jit(solution)/shard_map/all_to_all | solution.py:19
  154.8 13.2 %all_to_all.53 = f32[32,1,1]{2,1,0:T(1,128)S(1)} all-to-all(f32[32,1,1]{2,1,0:T(1,128)S(1)} %broadcast_in_dim.157), channel_id=1, replica_groups=mesh['slab_0'=4,'slab_1'=8,'col_0'=4,'col_1'=2] {'slab_0','slab_1'}, dimensions={0} | all-to-all | bytes 256 | tf_op jit(solution)/shard_map/all_to_all | solution.py:19
  170.5 1.3 collective-permute-start.17
  171.8 4.0 %collective-permute-start.16 = (f32[16,1,8,256]{3,0,2,1:T(8,128)S(1)}, f32[16,1,8,256]{3,0,2,1:T(8,128)S(1)}, u32[]{:S(2)}, u32[]{:S(2)}) collective-permute-start(f32[16,1,8,256]{3,0,2,1:T(8,128)S(1)} %get-tuple-element.24), channel_id=1, source_target_pairs={{0,8},{8,16},{16,24},{24,32},{32,40},{40,48},{48,56},{56,64},{64,7... | collective-permute-start | bytes 393224 | tf_op jit(solution)/shard_map/ppermute | solution.py:58
  175.9 4.6 %collective-permute-start.19 = (f32[16,8,1,256]{3,0,2,1:T(8,128)S(1)}, f32[16,8,1,256]{3,0,2,1:T(8,128)S(1)}, u32[]{:S(2)}, u32[]{:S(2)}) collective-permute-start(f32[16,8,1,256]{3,0,2,1:T(8,128)S(1)} %get-tuple-element.19), channel_id=1, source_target_pairs={{1,0},{2,1},{3,2},{4,3},{5,4},{6,5},{7,6},{9,8},{10,9},{11,10},{12... | collective-permute-start | bytes 393224 | tf_op jit(solution)/shard_map/ppermute | solution.py:59
  180.5 2.1 collective-permute-start.18
  183.5 1.0 collective-permute-done.18
  184.8 1.1 fusion.246
  187.2 9.1 %all_to_all.54 = f32[8,1,1]{2,1,0:T(1,128)S(1)} all-to-all(f32[8,1,1]{2,1,0:T(1,128)S(1)} %broadcast_in_dim.162), channel_id=1, replica_groups=mesh['slab_0'=4,'slab_1'=8,'col_0'=4,'col_1'=2] {'col_0','col_1'}, dimensions={0} | all-to-all | bytes 64 | tf_op jit(solution)/shard_map/all_to_all | solution.py:19
  197.6 13.2 %all_to_all.55 = f32[32,1,1]{2,1,0:T(1,128)S(1)} all-to-all(f32[32,1,1]{2,1,0:T(1,128)S(1)} %broadcast_in_dim.163), channel_id=1, replica_groups=mesh['slab_0'=4,'slab_1'=8,'col_0'=4,'col_1'=2] {'slab_0','slab_1'}, dimensions={0} | all-to-all | bytes 256 | tf_op jit(solution)/shard_map/all_to_all | solution.py:19
  212.4 1.6 copy.114
  (138 shorter events, 29.6 us)
Async XLA Ops:
  0.0 14.6 %copy-start = (f32[16,8,8,256]{3,2,1,0:T(8,128)S(1)}, f32[16,8,8,256]{3,2,1,0:T(8,128)}, u32[]{:S(2)}) copy-start(f32[16,8,8,256]{3,2,1,0:T(8,128)} %param.6) | copy-start | bytes 3145732
  0.8 25.7 %collective-permute-start = (f32[6,1,128]{2,0,1:T(8,128)S(1)}, f32[6,1,128]{2,0,1:T(8,128)S(1)}, u32[]{:S(2)}, u32[]{:S(2)}) collective-permute-start(f32[6,1,128]{2,0,1:T(8,128)S(1)} %copy.144), channel_id=1, source_target_pairs={{0,1},{1,2},{2,3},{3,4},{4,5},{5,6},{6,7},{8,9},{9,10},{10,11},{11... | collective-permute-start | bytes 9224 | tf_op jit(solution)/shard_map/ppermute | solution.py:41
  5.4 21.2 %collective-permute-start.1 = (f32[6,1,128]{2,0,1:T(8,128)S(1)}, f32[6,1,128]{2,0,1:T(8,128)S(1)}, u32[]{:S(2)}, u32[]{:S(2)}) collective-permute-start(f32[6,1,128]{2,0,1:T(8,128)S(1)} %copy.145), channel_id=1, source_target_pairs={{1,0},{2,1},{3,2},{4,3},{5,4},{6,5},{7,6},{9,8},{10,9},{11,10},{12... | collective-permute-start | bytes 9224 | tf_op jit(solution)/shard_map/ppermute | solution.py:43
  8.4 36.2 %collective-permute-start.4 = (f32[16,1,8,256]{3,0,2,1:T(8,128)S(1)}, f32[16,1,8,256]{3,0,2,1:T(8,128)}, u32[]{:S(2)}, u32[]{:S(2)}) collective-permute-start(f32[16,1,8,256]{3,0,2,1:T(8,128)S(1)} %copy.137), channel_id=1, source_target_pairs={{0,8},{8,16},{16,24},{24,32},{32,40},{40,48},{48,56},{56,64},{64,7... | collective-permute-start | bytes 393224 | tf_op jit(solution)/shard_map/ppermute | solution.py:58
  13.3 32.5 %collective-permute-start.5 = (f32[16,1,8,256]{3,0,2,1:T(8,128)}, f32[16,1,8,256]{3,0,2,1:T(8,128)}, u32[]{:S(2)}, u32[]{:S(2)}) collective-permute-start(f32[16,1,8,256]{3,0,2,1:T(8,128)} %copy.138), channel_id=1, source_target_pairs={{8,0},{16,8},{24,16},{32,24},{40,32},{48,40},{56,48},{64,56},{72,6... | collective-permute-start | bytes 393224 | tf_op jit(solution)/shard_map/ppermute | solution.py:59
  15.4 31.5 %collective-permute-start.6 = (f32[16,8,1,256]{3,0,1,2:T(8,128)}, f32[16,8,1,256]{3,0,1,2:T(8,128)}, u32[]{:S(2)}, u32[]{:S(2)}) collective-permute-start(f32[16,8,1,256]{3,0,1,2:T(8,128)} %copy.123), channel_id=1, source_target_pairs={{0,1},{1,2},{2,3},{3,4},{4,5},{5,6},{6,7},{8,9},{9,10},{10,11},{11... | collective-permute-start | bytes 393224 | tf_op jit(solution)/shard_map/ppermute | solution.py:58
  24.0 0.7 copy-start.10
  24.4 1.3 copy-start.6
  25.6 0.7 copy-start.9
  25.9 19.9 %copy-start.7 = (s32[16]{0:T(128)}, s32[16]{0:T(128)S(1)}, u32[]{:S(2)}) copy-start(s32[16]{0:T(128)S(1)} %get-tuple-element.8) | copy-start | bytes 196
  25.9 0.7 copy-start.5
  26.6 13.2 %collective-permute-start.3 = (f32[6,6,128]{2,0,1:T(8,128)S(1)}, f32[6,6,128]{2,0,1:T(8,128)S(1)}, u32[]{:S(2)}, u32[]{:S(2)}) collective-permute-start(f32[6,6,128]{2,0,1:T(8,128)S(1)} %constant_dynamic-update-slice_fusion), channel_id=1, source_target_pairs={{8,0},{16,8},{24,16},{32,24},{40,32},{48,40},{56,48},{64,56},{72,6... | collective-permute-start | bytes 55304 | tf_op jit(solution)/shard_map/ppermute | solution.py:43
  27.9 13.8 %collective-permute-start.2 = (f32[6,6,128]{2,0,1:T(8,128)S(1)}, f32[6,6,128]{2,0,1:T(8,128)S(1)}, u32[]{:S(2)}, u32[]{:S(2)}) collective-permute-start(f32[6,6,128]{2,0,1:T(8,128)S(1)} %constant_dynamic-update-slice_fusion), channel_id=1, source_target_pairs={{0,8},{8,16},{16,24},{24,32},{32,40},{40,48},{48,56},{56,64},{64,7... | collective-permute-start | bytes 55304 | tf_op jit(solution)/shard_map/ppermute | solution.py:41
  34.7 1.6 copy-start.3
  36.3 1.2 copy-start.2
  36.6 1.5 copy-start.1
  39.8 8.3 %collective-permute-start.7 = (f32[16,8,1,256]{3,0,1,2:T(8,128)S(1)}, f32[16,8,1,256]{3,0,1,2:T(8,128)S(1)}, u32[]{:S(2)}, u32[]{:S(2)}) collective-permute-start(f32[16,8,1,256]{3,0,1,2:T(8,128)S(1)} %copy.124), channel_id=1, source_target_pairs={{1,0},{2,1},{3,2},{4,3},{5,4},{6,5},{7,6},{9,8},{10,9},{11,10},{12... | collective-permute-start | bytes 393224 | tf_op jit(solution)/shard_map/ppermute | solution.py:59
  41.8 0.6 copy-start.14
  41.8 0.7 copy-start.15
  42.7 0.6 copy-start.12
  42.7 0.6 copy-start.13
  43.5 0.6 copy-start.11
  44.6 3.8 %copy-start.16 = (f32[8,8,256]{2,1,0:T(8,128)}, f32[8,8,256]{2,1,0:T(8,128)S(1)}, u32[]{:S(2)}) copy-start(f32[8,8,256]{2,1,0:T(8,128)S(1)} %get-tuple-element.60) | copy-start | bytes 196612
  48.4 1.6 copy-start.4
  84.9 12.0 %collective-permute-start.9 = (f32[16,1,8,256]{3,0,2,1:T(8,128)S(1)}, f32[16,1,8,256]{3,0,2,1:T(8,128)S(1)}, u32[]{:S(2)}, u32[]{:S(2)}) collective-permute-start(f32[16,1,8,256]{3,0,2,1:T(8,128)S(1)} %get-tuple-element.43), channel_id=1, source_target_pairs={{8,0},{16,8},{24,16},{32,24},{40,32},{48,40},{56,48},{64,56},{72,6... | collective-permute-start | bytes 393224 | tf_op jit(solution)/shard_map/ppermute | solution.py:59
  86.2 11.0 %collective-permute-start.8 = (f32[16,1,8,256]{3,0,2,1:T(8,128)S(1)}, f32[16,1,8,256]{3,0,2,1:T(8,128)S(1)}, u32[]{:S(2)}, u32[]{:S(2)}) collective-permute-start(f32[16,1,8,256]{3,0,2,1:T(8,128)S(1)} %get-tuple-element.44), channel_id=1, source_target_pairs={{0,8},{8,16},{16,24},{24,32},{32,40},{40,48},{48,56},{56,64},{64,7... | collective-permute-start | bytes 393224 | tf_op jit(solution)/shard_map/ppermute | solution.py:58
  90.2 6.7 %copy-start.8 = (s32[16]{0:T(128)S(1)}, s32[16]{0:T(128)}, u32[]{:S(2)}) copy-start(s32[16]{0:T(128)} %copy-done.7) | copy-start | bytes 196
  90.2 7.4 %collective-permute-start.11 = (f32[16,8,1,256]{3,0,2,1:T(8,128)S(1)}, f32[16,8,1,256]{3,0,2,1:T(8,128)S(1)}, u32[]{:S(2)}, u32[]{:S(2)}) collective-permute-start(f32[16,8,1,256]{3,0,2,1:T(8,128)S(1)} %get-tuple-element.39), channel_id=1, source_target_pairs={{1,0},{2,1},{3,2},{4,3},{5,4},{6,5},{7,6},{9,8},{10,9},{11,10},{12... | collective-permute-start | bytes 393224 | tf_op jit(solution)/shard_map/ppermute | solution.py:59
  94.8 4.0 %collective-permute-start.10 = (f32[16,8,1,256]{3,0,2,1:T(8,128)S(1)}, f32[16,8,1,256]{3,0,2,1:T(8,128)S(1)}, u32[]{:S(2)}, u32[]{:S(2)}) collective-permute-start(f32[16,8,1,256]{3,0,2,1:T(8,128)S(1)} %get-tuple-element.40), channel_id=1, source_target_pairs={{0,1},{1,2},{2,3},{3,4},{4,5},{5,6},{6,7},{8,9},{9,10},{10,11},{11... | collective-permute-start | bytes 393224 | tf_op jit(solution)/shard_map/ppermute | solution.py:58
  97.9 1.2 copy-start.17
  127.8 12.0 %collective-permute-start.13 = (f32[16,1,8,256]{3,0,2,1:T(8,128)S(1)}, f32[16,1,8,256]{3,0,2,1:T(8,128)S(1)}, u32[]{:S(2)}, u32[]{:S(2)}) collective-permute-start(f32[16,1,8,256]{3,0,2,1:T(8,128)S(1)} %get-tuple-element.33), channel_id=1, source_target_pairs={{8,0},{16,8},{24,16},{32,24},{40,32},{48,40},{56,48},{64,56},{72,6... | collective-permute-start | bytes 393224 | tf_op jit(solution)/shard_map/ppermute | solution.py:59
  129.1 11.0 %collective-permute-start.12 = (f32[16,1,8,256]{3,0,2,1:T(8,128)S(1)}, f32[16,1,8,256]{3,0,2,1:T(8,128)S(1)}, u32[]{:S(2)}, u32[]{:S(2)}) collective-permute-start(f32[16,1,8,256]{3,0,2,1:T(8,128)S(1)} %get-tuple-element.34), channel_id=1, source_target_pairs={{0,8},{8,16},{16,24},{24,32},{32,40},{40,48},{48,56},{56,64},{64,7... | collective-permute-start | bytes 393224 | tf_op jit(solution)/shard_map/ppermute | solution.py:58
  133.1 7.4 %collective-permute-start.15 = (f32[16,8,1,256]{3,0,2,1:T(8,128)S(1)}, f32[16,8,1,256]{3,0,2,1:T(8,128)S(1)}, u32[]{:S(2)}, u32[]{:S(2)}) collective-permute-start(f32[16,8,1,256]{3,0,2,1:T(8,128)S(1)} %get-tuple-element.29), channel_id=1, source_target_pairs={{1,0},{2,1},{3,2},{4,3},{5,4},{6,5},{7,6},{9,8},{10,9},{11,10},{12... | collective-permute-start | bytes 393224 | tf_op jit(solution)/shard_map/ppermute | solution.py:59
  137.7 4.0 %collective-permute-start.14 = (f32[16,8,1,256]{3,0,2,1:T(8,128)S(1)}, f32[16,8,1,256]{3,0,2,1:T(8,128)S(1)}, u32[]{:S(2)}, u32[]{:S(2)}) collective-permute-start(f32[16,8,1,256]{3,0,2,1:T(8,128)S(1)} %get-tuple-element.30), channel_id=1, source_target_pairs={{0,1},{1,2},{2,3},{3,4},{4,5},{5,6},{6,7},{8,9},{9,10},{10,11},{11... | collective-permute-start | bytes 393224 | tf_op jit(solution)/shard_map/ppermute | solution.py:58
  170.5 12.0 %collective-permute-start.17 = (f32[16,1,8,256]{3,0,2,1:T(8,128)S(1)}, f32[16,1,8,256]{3,0,2,1:T(8,128)S(1)}, u32[]{:S(2)}, u32[]{:S(2)}) collective-permute-start(f32[16,1,8,256]{3,0,2,1:T(8,128)S(1)} %get-tuple-element.23), channel_id=1, source_target_pairs={{8,0},{16,8},{24,16},{32,24},{40,32},{48,40},{56,48},{64,56},{72,6... | collective-permute-start | bytes 393224 | tf_op jit(solution)/shard_map/ppermute | solution.py:59
  171.8 11.0 %collective-permute-start.16 = (f32[16,1,8,256]{3,0,2,1:T(8,128)S(1)}, f32[16,1,8,256]{3,0,2,1:T(8,128)S(1)}, u32[]{:S(2)}, u32[]{:S(2)}) collective-permute-start(f32[16,1,8,256]{3,0,2,1:T(8,128)S(1)} %get-tuple-element.24), channel_id=1, source_target_pairs={{0,8},{8,16},{16,24},{24,32},{32,40},{40,48},{48,56},{56,64},{64,7... | collective-permute-start | bytes 393224 | tf_op jit(solution)/shard_map/ppermute | solution.py:58
  175.9 7.4 %collective-permute-start.19 = (f32[16,8,1,256]{3,0,2,1:T(8,128)S(1)}, f32[16,8,1,256]{3,0,2,1:T(8,128)S(1)}, u32[]{:S(2)}, u32[]{:S(2)}) collective-permute-start(f32[16,8,1,256]{3,0,2,1:T(8,128)S(1)} %get-tuple-element.19), channel_id=1, source_target_pairs={{1,0},{2,1},{3,2},{4,3},{5,4},{6,5},{7,6},{9,8},{10,9},{11,10},{12... | collective-permute-start | bytes 393224 | tf_op jit(solution)/shard_map/ppermute | solution.py:59
  180.5 4.0 %collective-permute-start.18 = (f32[16,8,1,256]{3,0,2,1:T(8,128)S(1)}, f32[16,8,1,256]{3,0,2,1:T(8,128)S(1)}, u32[]{:S(2)}, u32[]{:S(2)}) collective-permute-start(f32[16,8,1,256]{3,0,2,1:T(8,128)S(1)} %get-tuple-element.20), channel_id=1, source_target_pairs={{0,1},{1,2},{2,3},{3,4},{4,5},{5,6},{6,7},{8,9},{9,10},{10,11},{11... | collective-permute-start | bytes 393224 | tf_op jit(solution)/shard_map/ppermute | solution.py:58
where the time goes:
time: 215 us; the launch traced here: 214 us
  blocking collectives  96.3 us (45%)
  starting transfers between devices  59.9 us (28%)
  local copies, waits for them, and re-layouts  23.5 us (11%)
  other arithmetic  19 us (9%)
  matrix products  7.67 us (4%)
  between operations  4.15 us (2%)
  waiting for transfers between devices  3.38 us (2%)
    all_to_all x8, blocking collectives, sent_to_all(): return lax.all_to_all(copies, axis, split_axis=0, concat_axis=0, tiled=True)  96.3 us
    ppermute x8, starting transfers between devices, with_halo(): lax.ppermute(last, axis, up)  26.4 us
    ppermute x8, starting transfers between devices, with_halo(): lax.ppermute(first, axis, [(b, a) for a, b in up])  20.9 us
    ppermute x2, starting transfers between devices, padded_2(): lax.ppermute(tail, axis, [(i, (i + 1) % count) for i in range(ends)])  9.48 us
    unnamed x50, local copies, waits for them, and re-layouts  9.11 us
    dot_general x16, matrix products, apply_slots(): jnp.einsum('qr,ryz->qyz', matrix, face_cells, precision=FULL_ACCURACY)  6.78 us
    sub x4, other arithmetic, rates(): squares - fields * fields  4.93 us
  transfers between devices with their start and end apart: 20, of which 6 were waited for; matrix products, arithmetic and copies ran while one was open for 10% of the time, Pallas kernels for 0%

commit v1 on v0

v1 whole, which is shorter than its diff:
```python
import functools

import jax
import jax.numpy as jnp
from jax import lax
from jax.experimental import pallas as pl
from jax.experimental.pallas import tpu as pltpu
from jax.sharding import PartitionSpec as P

Q = 16
G = 4
CX = 8
CY = 8
NZ = 256
CAP = 6
CYC = 4
NZC = 128
TIME_STEP = 0.05
EXACT = lax.Precision.HIGHEST
MESH = pl.DeviceIdType.MESH
F32 = jnp.float32
I32 = jnp.int32


def near(face):
    return 1 if face in (0, 2) else 0


def kernel(
    torus,
    rows_s,
    ids_s,
    energy_s,
    fields_hbm,
    mask_hbm,
    coarse_hbm,
    out_ref,
    raw,
    mask,
    cb,
    pb,
    u_ref,
    v_ref,
    bf,
    nbi,
    rm,
    ym,
    yf,
    rf,
    ya,
    ra,
    st,
    ys,
    rs,
    hy,
    y2,
    r2,
    ar_src,
    ar_rcv,
    e_s,
    perm_s,
    pos_s,
    local_sem,
    send_sem,
    recv_sem,
):
    nx, nzt, ny, nk = torus
    slabs, cols = nx * nzt, ny * nk
    s = lax.axis_index("slab")
    c = lax.axis_index("col")
    tx, tz = s // nzt, s % nzt
    ty, tk = c // nk, c % nk
    planes_all = slabs * (CX // 2)
    rows_all = cols * CYC

    local = [
        pltpu.make_async_copy(coarse_hbm, cb.at[pl.ds(4 * CAP, CAP)], local_sem.at[0]),
        pltpu.make_async_copy(mask_hbm, mask, local_sem.at[1]),
        pltpu.make_async_copy(fields_hbm, raw, local_sem.at[2]),
    ]
    for copy in local:
        copy.start()

    def halo_peer(ds, dc):
        return ((s + ds + slabs) % slabs, (c + dc + cols) % cols)

    def peer_1(dz, dk):
        return (tx * nzt + (tz + dz) % nzt, ty * nk + (tk + dk) % nk)

    def peer_2(dx, dy):
        return (((tx + dx) % nx) * nzt + tz, ((ty + dy) % ny) * nk + tk)

    halo_offsets = [(a, b) for a in (-1, 0, 1) for b in (-1, 0, 1) if (a, b) != (0, 0)]
    group_1 = [(a, b) for a in range(nzt) for b in range(nk) if (a, b) != (0, 0)]
    group_2 = [(a, b) for a in range(nx) for b in range(ny) if (a, b) != (0, 0)]
    group_1.sort(key=lambda o: -min(o[0], nzt - o[0]))
    group_2.sort(key=lambda o: -(min(o[0], nx - o[0]) + min(o[1], ny - o[1])))
    peers = [halo_peer(*o) for o in halo_offsets]
    peers += [peer_1(*o) for o in group_1] + [peer_2(*o) for o in group_2]
    barrier = pltpu.get_barrier_semaphore()
    for peer in peers:
        pl.semaphore_signal(barrier, inc=1, device_id=peer, device_id_type=MESH)

    face_offset = ((-1, 0), (1, 0), (0, -1), (0, 1))
    has_flag = (s > 0, s < slabs - 1, c > 0, c < cols - 1)
    has = [jnp.where(flag, 1.0, 0.0).astype(F32) for flag in has_flag]

    count = [0]

    def send(src, dst, peer):
        at = count[0]
        count[0] += 1
        copy = pltpu.make_async_remote_copy(
            src_ref=src,
            dst_ref=dst,
            send_sem=send_sem.at[at],
            recv_sem=recv_sem.at[at],
            device_id=peer,
            device_id_type=MESH,
        )
        copy.start()
        return copy

    own = [ids_s[s, c, q] for q in range(Q)]
    group = [jnp.int32(-1)] * Q
    for face, (ds, dc) in enumerate(face_offset):
        sn = jnp.clip(s + ds, 0, slabs - 1)
        cn = jnp.clip(c + dc, 0, cols - 1)

        def match(r, found, sn=sn, cn=cn, face=face):
            other = jnp.where(has_flag[face], ids_s[sn, cn, r], -1)
            return tuple(jnp.where(o == other, face, g) for o, g in zip(own, found))

        group = lax.fori_loop(0, Q, match, tuple(group))
    first_free = jnp.where(s == 0, 0, jnp.where(s == slabs - 1, 1, jnp.where(c == 0, 2, 3)))
    last_free = jnp.where(c == 0, 2, 3)
    key = []
    for q in range(Q):
        free_rank = jnp.int32(0)
        for p in range(Q):
            if p != q:
                free_rank += jnp.where((group[p] < 0) & (own[p] < own[q]), 1, 0)
        place = jnp.where(free_rank < G, first_free, last_free)
        key.append(jnp.where(group[q] < 0, place, group[q]) * 65536 + own[q])
    for q in range(Q):
        rank = jnp.int32(0)
        for p in range(Q):
            if p != q:
                rank += jnp.where(key[p] < key[q], 1, 0)
        pos_s[q] = rank
    for p in range(Q):
        slot = jnp.int32(0)
        for q in range(1, Q):
            slot = jnp.where(pos_s[q] == p, q, slot)
        perm_s[p] = slot
        e_s[p] = energy_s[ids_s[s, c, slot]]
    e_total = e_s[0]
    for p in range(1, Q):
        e_total += e_s[p]

    start_own = jnp.int32(0)
    for i in range(slabs):
        start_own += jnp.where(i < s, rows_s[i], 0)
    end_own = start_own + rows_s[s]
    start_prev = start_own - rows_s[jnp.maximum(s - 1, 0)]

    zero_slab = jnp.zeros((CY, NZ), F32)
    for q in range(Q):
        for ref in (u_ref, v_ref):
            if q // G != 0:
                ref[q, 0:8, :] = zero_slab
            if q // G != 1:
                ref[q, 72:80, :] = zero_slab

    sub = lax.broadcasted_iota(I32, (CY, NZ), 0)
    lane = lax.broadcasted_iota(I32, (CY, NZ), 1)

    def column(view, start):
        rows = jnp.broadcast_to(view[pl.ds(start, 1), :], (CX, NZ))
        for x in range(1, CX):
            rows = jnp.where(sub == x, view[pl.ds(start + CY * x, 1), :], rows)
        return rows

    out_row = lax.broadcasted_iota(I32, (128, 64), 0)
    in_row = lax.broadcasted_iota(I32, (128, 64), 1)
    high = out_row >> 3
    low = out_row & 7
    along = jnp.where(
        out_row < 64,
        high,
        jnp.where(out_row < 80, high - 10, jnp.where(out_row < 96, high - 2, low)),
    )
    across = jnp.where(
        out_row < 96, low, jnp.where(out_row < 112, high - 14, high - 6)
    )

    def node_weight(fine, node):
        twice = 2 * fine - 1
        lower = twice >> 2
        w = (twice - 4 * lower).astype(F32) * 0.25
        return jnp.where(node == lower + 2, 1.0 - w, jnp.where(node == lower + 3, w, 0.0))

    weight_xy = node_weight(along, in_row >> 3) * node_weight(across, in_row & 7)
    node_z = lax.broadcasted_iota(I32, (NZC, NZ), 0)
    fine_z = lax.broadcasted_iota(I32, (NZC, NZ), 1)
    lower_z = (2 * fine_z - 1) >> 2
    w_z = (2 * fine_z - 1 - 4 * lower_z).astype(F32) * 0.25
    weight_z = jnp.where(node_z == jnp.clip(lower_z, 0, NZC - 1), 1.0 - w_z, 0.0) + jnp.where(
        node_z == jnp.clip(lower_z + 1, 0, NZC - 1), w_z, 0.0
    )

    local[1].wait()
    for k in range(2):
        ym[0, 8 * k : 8 * k + 8, :] = column(mask, k)
        ym[1, 8 * k : 8 * k + 8, :] = column(mask, 6 + k)
    local[2].wait()
    for p in range(Q):
        u_ref[p, 8:72, :] = raw[perm_s[p]]
    for j in range(G):
        yf[0, j] = column(u_ref.at[2 * G + j], 8)
        yf[1, j] = column(u_ref.at[3 * G + j], 15)
    local[0].wait()

    pl.semaphore_wait(barrier, len(peers))

    first = []
    for ds, dc in halo_offsets:
        slot = (1 - dc) * 3 + (1 - ds)
        first.append(
            send(
                cb.at[pl.ds(4 * CAP, CAP)], cb.at[pl.ds(slot * CAP, CAP)], halo_peer(ds, dc)
            )
        )
    mask_src = (mask.at[pl.ds(0, 16)], mask.at[pl.ds(48, 16)], ym.at[0], ym.at[1])
    field_src = (
        u_ref.at[pl.ds(0, G), pl.ds(8, 8)],
        u_ref.at[pl.ds(G, G), pl.ds(64, 8)],
        yf.at[0],
        yf.at[1],
    )
    mask_copies = []
    field_copies = []
    for face in range(4):
        mask_copies.append(send(mask_src[face], rm.at[face ^ 1], halo_peer(*face_offset[face])))
    for face in range(4):
        field_copies.append(send(field_src[face], rf.at[face ^ 1], halo_peer(*face_offset[face])))

    for copy in first:
        copy.wait_recv()
    for i in range(8):
        plane = jnp.clip(s * (CX // 2) - 2 + i, 0, planes_all - 1)
        flat = jnp.where(
            plane < start_own,
            plane - start_prev,
            jnp.where(plane < end_own, CAP + plane - start_own, 2 * CAP + plane - end_own),
        )
        flat = jnp.clip(flat, 0, 3 * CAP - 1)
        mine = cb[3 * CAP + flat]
        left = cb[flat, CYC - 2 : CYC, :]
        right = cb[6 * CAP + flat, 0:2, :]
        pb[8 * i : 8 * i + 2, :] = jnp.where(c == 0, mine[0:1], left)
        pb[8 * i + 2 : 8 * i + 6, :] = mine
        pb[8 * i + 6 : 8 * i + 8, :] = jnp.where(c == cols - 1, mine[CYC - 1 : CYC], right)
    profile = jnp.dot(weight_xy, pb[...], precision=EXACT, preferred_element_type=F32)
    profile = jnp.dot(profile, weight_z, precision=EXACT, preferred_element_type=F32)
    scaled = TIME_STEP * jnp.exp(2.0 * (profile - 1.0))
    bf[0:64, :] = scaled[0:64] * mask[...].astype(F32)
    for copy in mask_copies:
        copy.wait_recv()
    for face in range(4):
        at = 64 + 16 * face
        bf[at : at + 16, :] = scaled[at : at + 16] * rm[face].astype(F32) * has[face]

    def near_b(face):
        at = 64 + 16 * face + 8 * near(face)
        return bf[at : at + 8, :]

    def sides(f, low_row, high_row):
        total = jnp.where(sub == 0, low_row, pltpu.roll(f, 1, 0))
        total += jnp.where(sub == CY - 1, high_row, pltpu.roll(f, CY - 1, 0))
        total += jnp.where(lane == 0, 0.0, pltpu.roll(f, 1, 1))
        total += jnp.where(lane == NZ - 1, 0.0, pltpu.roll(f, NZ - 1, 1))
        return total

    sum_b = zero_slab
    sum_b4 = zero_slab
    sum_bnb = zero_slab
    for x in range(CX):
        b = bf[8 * x : 8 * x + 8, :]
        around = sides(b, 0.0, 0.0)
        if x > 0:
            around += bf[8 * x - 8 : 8 * x, :]
        if x < CX - 1:
            around += bf[8 * x + 8 : 8 * x + 16, :]
        nbi[8 * x : 8 * x + 8, :] = around
        square = b * b
        sum_b += b
        sum_b4 += square * square
        sum_bnb += 16.0 * b * around
    face_b = (
        bf[0:8, :],
        bf[56:64, :],
        column(bf, 0),
        column(bf, 7),
    )
    for face in range(4):
        sum_bnb += 4.0 * face_b[face] * near_b(face)

    for copy in field_copies:
        copy.wait_recv()
    for j in range(G):
        u_ref[j, 0:8, :] = rf[0, j] * has[0]
        u_ref[G + j, 72:80, :] = rf[1, j] * has[1]
        hy[0, j] = rf[2, j] * has[2]
        hy[1, j] = rf[3, j] * has[3]

    def stencil(src, dst, shift, sums):
        def body(x, carry):
            r = pl.multiple_of(8 * x, 8)
            b = bf[pl.ds(r, 8), :]
            squares = zero_slab
            for q in range(Q):
                f = src[q, pl.ds(r + 8, 8), :]
                squares += f * f
            common = 5.0 + 3.0 * squares
            force_all = zero_slab
            t1 = zero_slab
            t2 = zero_slab
            t3 = zero_slab
            te = zero_slab
            te2 = zero_slab
            for q in range(Q):
                e = e_s[q]
                f = src[q, pl.ds(r + 8, 8), :]
                low_row = hy[0, q - 2 * G, pl.ds(x, 1), :] if q // G == 2 else 0.0
                high_row = hy[1, q - 3 * G, pl.ds(x, 1), :] if q // G == 3 else 0.0
                around = src[q, pl.ds(r, 8), :] + src[q, pl.ds(r + 16, 8), :]
                around += sides(f, low_row, high_row)
                force = f * ((common - e) + f * (e - 2.0 * f)) - around
                if sums:
                    a = f - b * force
                    force_all += force
                    square = a * a
                    ea = e * a
                    t1 += a
                    t2 += square
                    t3 += square * a
                    te += ea
                    te2 += ea * a
                else:
                    a = f - b * (force + shift)
                dst[q, pl.ds(r + 8, 8), :] = a
            if not sums:
                return carry
            st[0, pl.ds(r, 8), :] = t2
            st[1, pl.ds(r, 8), :] = t1
            total, k0, k1, k2 = carry
            b2 = b * b
            total += b * force_all
            k0 += b * (t1 * (5.0 + 3.0 * t2) - te + te2 - 2.0 * t3) - t1 * nbi[pl.ds(r, 8), :]
            k1 += b2 * (e_total - 80.0 - 42.0 * t2 - 6.0 * t1 * t1 - 2.0 * te)
            k2 += b2 * b * (138.0 * t1 + e_total)
            return total, k0, k1, k2

        start = (zero_slab,) * 4 if sums else 0
        return lax.fori_loop(0, CX, body, start)

    def face_sum(k0):
        for j in range(G):
            k0 -= v_ref[j, 8:16, :] * near_b(0)
            k0 -= v_ref[G + j, 64:72, :] * near_b(1)
            k0 -= column(v_ref.at[2 * G + j], 8) * near_b(2)
            k0 -= column(v_ref.at[3 * G + j], 15) * near_b(3)
        return k0

    lane_1 = lax.broadcasted_iota(I32, (1, 128), 1)

    def put_row(at, parts):
        row = jnp.zeros((1, 128), F32)
        for k, part in enumerate(parts):
            value = jnp.sum(jnp.sum(part, axis=0, keepdims=True), axis=1, keepdims=True)
            row += jnp.where(lane_1 == k, value, 0.0)
        ar_src[at] = row

    def spread(at, offsets, peer_of):
        return [
            send(ar_src.at[at], ar_rcv.at[at, k], peer_of(*offset))
            for k, offset in enumerate(offsets)
        ]

    def gathered(at, copies):
        for copy in copies:
            copy.wait_recv()
        row = ar_src[at]
        for k in range(len(copies)):
            row += ar_rcv[at, k]
        return row

    def two_multipliers(row):
        got = [
            jnp.sum(jnp.where(lane_1 == k, row, 0.0), axis=1, keepdims=True) for k in range(6)
        ]
        inverse = -1.0 / (16.0 * got[0])
        m_a = got[1] * inverse
        m_b = (got[2] + m_a * (got[3] + m_a * (got[4] + m_a * got[5]))) * inverse
        return jnp.broadcast_to(m_a, (CY, NZ)), jnp.broadcast_to(m_b, (CY, NZ))

    def all_sums(at, parts, between):
        total, k0, k1, k2 = parts
        put_row(at, (sum_b, total, face_sum(k0), k1 + sum_bnb, k2, -736.0 * sum_b4))
        copies = spread(at, group_1, peer_1)
        extra = between()
        ar_src[at + 1] = gathered(at, copies)
        more = spread(at + 1, group_2, peer_2)
        result = two_multipliers(gathered(at + 1, more))
        return result, extra, copies + more

    parts = stencil(u_ref, v_ref, None, True)

    def send_deep():
        copies = []
        for j in range(G):
            for k in range(2):
                ya[0, j, 8 * k : 8 * k + 8, :] = column(v_ref.at[2 * G + j], 8 + k)
                ya[1, j, 8 * k : 8 * k + 8, :] = column(v_ref.at[3 * G + j], 14 + k)
        for k in range(2):
            ys[0, k] = column(st.at[k], 0)
            ys[1, k] = column(st.at[k], 7)
        deep = (
            v_ref.at[pl.ds(0, G), pl.ds(8, 16)],
            v_ref.at[pl.ds(G, G), pl.ds(56, 16)],
            ya.at[0],
            ya.at[1],
        )
        flat = (st.at[:, pl.ds(0, 8)], st.at[:, pl.ds(56, 8)], ys.at[0], ys.at[1])
        for face in range(4):
            peer = halo_peer(*face_offset[face])
            copies.append(send(deep[face], ra.at[face ^ 1], peer))
            copies.append(send(flat[face], rs.at[face ^ 1], peer))
        return copies

    (m0, m1), deep_copies, sent_1 = all_sums(0, parts, send_deep)

    for copy in field_copies:
        copy.wait_send()
    for copy in deep_copies:
        copy.wait()

    def settle(m):
        def body(x, carry):
            r = pl.multiple_of(8 * x, 8)
            mb = m * bf[pl.ds(r, 8), :]
            for q in range(Q):
                v_ref[q, pl.ds(r + 8, 8), :] = v_ref[q, pl.ds(r + 8, 8), :] - mb
            return carry

        lax.fori_loop(0, CX, body, 0)

    settle(m0)
    for face in range(4):
        at = 64 + 16 * face
        for k in range(2):
            mb = m0 * bf[at + 8 * k : at + 8 * k + 8, :]
            for j in range(G):
                value = ra[face, j, 8 * k : 8 * k + 8, :] * has[face] - mb
                ra[face, j, 8 * k : 8 * k + 8, :] = value
                if k == near(face):
                    if face == 0:
                        v_ref[j, 0:8, :] = value
                    elif face == 1:
                        v_ref[G + j, 72:80, :] = value
                    else:
                        hy[face - 2, j] = value

    for face in range(4):
        b = near_b(face)
        mb = m0 * b
        squares = rs[face, 0] - 2.0 * mb * rs[face, 1] + 16.0 * mb * mb
        common = 5.0 + 3.0 * squares
        here, beyond = 8 * near(face), 8 * (1 - near(face))
        for j in range(G):
            q = face * G + j
            e = e_s[q]
            f = ra[face, j, here : here + 8, :]
            if face == 0:
                inner = v_ref[q, 8:16, :]
            elif face == 1:
                inner = v_ref[q, 64:72, :]
            elif face == 2:
                inner = column(v_ref.at[q], 8)
            else:
                inner = column(v_ref.at[q], 15)
            around = ra[face, j, beyond : beyond + 8, :] + inner + sides(f, 0.0, 0.0)
            force = f * ((common - e) + f * (e - 2.0 * f)) - around
            value = f - b * (force + m1)
            if face == 0:
                u_ref[j, 0:8, :] = value
            elif face == 1:
                u_ref[G + j, 72:80, :] = value
            else:
                y2[face - 2, j] = value
    stencil(v_ref, u_ref, m1, False)
    for j in range(G):
        hy[0, j] = y2[0, j]
        hy[1, j] = y2[1, j]

    parts = stencil(u_ref, v_ref, None, True)

    def send_shallow():
        for j in range(G):
            y2[0, j] = column(v_ref.at[2 * G + j], 8)
            y2[1, j] = column(v_ref.at[3 * G + j], 15)
        source = (
            v_ref.at[pl.ds(0, G), pl.ds(8, 8)],
            v_ref.at[pl.ds(G, G), pl.ds(64, 8)],
            y2.at[0],
            y2.at[1],
        )
        return [
            send(source[face], r2.at[face ^ 1], halo_peer(*face_offset[face]))
            for face in range(4)
        ]

    (m2, m3), shallow_copies, sent_2 = all_sums(2, parts, send_shallow)
    for copy in shallow_copies:
        copy.wait()
    settle(m2)
    mb = [m2 * near_b(face) for face in range(4)]
    for j in range(G):
        v_ref[j, 0:8, :] = r2[0, j] * has[0] - mb[0]
        v_ref[G + j, 72:80, :] = r2[1, j] * has[1] - mb[1]
        hy[0, j] = r2[2, j] * has[2] - mb[2]
        hy[1, j] = r2[3, j] * has[3] - mb[3]
    stencil(v_ref, u_ref, m3, False)
    for q in range(Q):
        out_ref[q] = u_ref[pos_s[q], 8:72, :]
    for copy in first + mask_copies + sent_1 + sent_2:
        copy.wait_send()


def per_device(torus, order_params, layer_mask, coarse_temp, coarse_rows, grain_ids, energy):
    any_space = pl.BlockSpec(memory_space=pl.ANY)
    smem = pl.BlockSpec(memory_space=pltpu.SMEM)
    vmem = pl.BlockSpec(memory_space=pltpu.VMEM)
    nx, nzt, ny, nk = torus
    copies = 16 + 8 + 4 + 2 * (nzt * nk - 1 + nx * ny - 1)
    slots = max(nzt * nk, nx * ny)
    rows = CX * CY
    out = pl.pallas_call(
        functools.partial(kernel, torus),
        out_shape=jax.ShapeDtypeStruct((Q, rows, NZ), F32),
        in_specs=[smem] * 3 + [any_space] * 3,
        out_specs=vmem,
        scratch_shapes=[
            pltpu.VMEM((Q, rows, NZ), F32),
            pltpu.VMEM((rows, NZ), I32),
            pltpu.VMEM((9 * CAP, CYC, NZC), F32),
            pltpu.VMEM((64, NZC), F32),
            pltpu.VMEM((Q, rows + 16, NZ), F32),
            pltpu.VMEM((Q, rows + 16, NZ), F32),
            pltpu.VMEM((128, NZ), F32),
            pltpu.VMEM((rows, NZ), F32),
            pltpu.VMEM((4, 16, NZ), I32),
            pltpu.VMEM((2, 16, NZ), I32),
            pltpu.VMEM((2, G, 8, NZ), F32),
            pltpu.VMEM((4, G, 8, NZ), F32),
            pltpu.VMEM((2, G, 16, NZ), F32),
            pltpu.VMEM((4, G, 16, NZ), F32),
            pltpu.VMEM((2, rows, NZ), F32),
            pltpu.VMEM((2, 2, 8, NZ), F32),
            pltpu.VMEM((4, 2, 8, NZ), F32),
            pltpu.VMEM((2, G, 8, NZ), F32),
            pltpu.VMEM((2, G, 8, NZ), F32),
            pltpu.VMEM((4, G, 8, NZ), F32),
            pltpu.VMEM((4, 1, 128), F32),
            pltpu.VMEM((4, slots, 1, 128), F32),
            pltpu.SMEM((Q,), F32),
            pltpu.SMEM((Q,), I32),
            pltpu.SMEM((Q,), I32),
            pltpu.SemaphoreType.DMA((3,)),
            pltpu.SemaphoreType.DMA((copies,)),
            pltpu.SemaphoreType.DMA((copies,)),
        ],
        compiler_params=pltpu.CompilerParams(collective_id=0, has_side_effects=True),
    )(
        coarse_rows,
        grain_ids,
        energy,
        order_params.reshape(Q, rows, NZ),
        layer_mask.reshape(rows, NZ),
        coarse_temp,
    )
    return out.reshape(Q, CX, CY, NZ)


def solution(mesh, torus=(4, 8, 4, 2)):
    placed = (
        P(None, "slab", "col", None),
        P("slab", "col", None),
        P("slab", "col", None),
        P(),
        P(),
        P(),
    )
    return jax.shard_map(
        functools.partial(per_device, torus),
        mesh=mesh,
        in_specs=placed,
        out_specs=P(None, "slab", "col", None),
        check_vma=False,
    )
```

time: 215 us -> 50 us (0.23)
  blocking collectives: 96.3 us -> 0 us
  starting transfers between devices: 59.9 us -> 0 us
  Pallas kernels: 0 us -> 45.9 us
  local copies, waits for them, and re-layouts: 23.5 us -> 3.89 us
  other arithmetic: 19 us -> 0 us
  matrix products: 7.67 us -> 0 us
  between operations: 4.15 us -> 0.01 us
  waiting for transfers between devices: 3.38 us -> 0 us
    all_to_all x8 -> x0, blocking collectives: 96.3 us -> none  [sent_to_all(): return lax.all_to_all(copies, axis, split_axis=0, concat_axis=0, tiled=True)]
    ppermute x20 -> x0, starting transfers between devices: 59.9 us -> none  [the longest x8 26.4 us: with_halo(): lax.ppermute(last, axis, up)]
    pallas_call x0 -> x1, Pallas kernels: none -> 45.9 us  [per_device(): pl.pallas_call(functools.partial(kernel, torus), out_shape=jax.ShapeDtype...]
    slice x22 -> x0, local copies, waits for them, and re-layouts: 8.54 us -> none  [the longest x4 2.27 us: per_device(): y_high = jnp.concatenate([fields[:, :, 1:], right_side[:, :, None]], axis=2)]
    dot_general x19 -> x0, matrix products: 7.67 us -> none  [the longest x16 6.78 us: apply_slots(): jnp.einsum('qr,ryz->qyz', matrix, face_cells, precision=FULL_ACCURACY)]
    reduce_sum x14 -> x0, other arithmetic: 7.28 us -> none  [the longest x8 3.81 us: taken_together(): return jnp.sum(everything, axis=0)]
    sub x6 -> x0, other arithmetic: 5.49 us -> none  [the longest x4 4.93 us: rates(): squares - fields * fields]
    unnamed x50 -> x2, local copies, waits for them, and re-layouts: 9.11 us -> 3.89 us
  transfers between devices with their start and end apart: 20 -> 0, of which waited for: 6 -> 0; matrix products, arithmetic and copies ran while one was open for 10% -> 0% of each run, Pallas kernels for 0% -> 0%
where the time goes in v1:
time: 50 us; the launch traced here: 49.8 us
  Pallas kernels  45.9 us (92%)
  local copies, waits for them, and re-layouts  3.89 us (8%)
    pallas_call x1, Pallas kernels, per_device(): pl.pallas_call(functools.partial(kernel, torus), out_shape=jax.ShapeDtype...  45.9 us
    unnamed x2, local copies, waits for them, and re-layouts  3.89 us

profile of v1, /device:TPU:1, one launch (start us, length us, event | category | flops | bytes accessed | tf_op | source)
XLA Modules:
  0.0 49.8 jit_solution(739077878209105664)
XLA Ops:
  0.0 1.6 %copy.7.ids_s = s32[32,8,16]{2,1,0:T(8,128)} copy(s32[32,8,16]{0,2,1:T(8,128)} %param.10) | data formatting | bytes 32768 | tf_op args[4]
  1.6 45.9 %shard_map.64 = f32[16,64,256]{2,1,0:T(8,128)} custom-call(s32[32]{0:T(128)} %rows_s.1, s32[32,8,16]{2,1,0:T(8,128)} %copy.7.ids_s, f32[2208]{0:T(1024)} %energy_s.1, f32[16,64,256]{2,1,0:T(8,128)} %bitcast.4, s32[64,256]{1,0:T(8,128)} %bitcast.5, f32[6,4,128]{2,1,0:T(4,128)} %coarse_hbm.1), custom_call_target="tpu_custom_call" | custom-call | tf_op jit(solution)/shard_map/pallas_call | solution.py:549
  47.5 2.3 %copy.9 = f32[16,8,8,256]{3,2,1,0:T(8,128)} copy(f32[16,8,8,256]{3,2,1,0:T(8,128)} %bitcast.3) | data formatting | bytes 2097152

commit v2 on v1

v2 whole, which is shorter than its diff:
```python
import functools

import jax
import jax.numpy as jnp
from jax import lax
from jax.experimental import pallas as pl
from jax.experimental.pallas import tpu as pltpu
from jax.sharding import PartitionSpec as P

Q = 16
G = 4
CX = 8
CY = 8
NZ = 256
CAP = 6
CYC = 4
NZC = 128
TIME_STEP = 0.05
EXACT = lax.Precision.HIGHEST
MESH = pl.DeviceIdType.MESH
F32 = jnp.float32
I32 = jnp.int32


def near(face):
    return 1 if face in (0, 2) else 0


def wait_for(ref, sem):
    pltpu.make_async_copy(ref, ref, sem).wait()


def kernel(
    torus,
    rows_hbm,
    ids_hbm,
    energy_hbm,
    fields_hbm,
    mask_hbm,
    coarse_hbm,
    out_ref,
    pos_s,
    raw,
    mask,
    cb,
    cl,
    cr,
    pb,
    u_ref,
    v_ref,
    bf,
    nbi,
    nbg,
    rm,
    ym,
    yf,
    rf,
    ya,
    ra,
    st,
    ys,
    rs,
    sq,
    hy,
    ah,
    nh,
    nbh,
    y2,
    r2,
    ar_src,
    ar_1a,
    ar_1b,
    ar_2a,
    ar_2b,
    rows_s,
    ids_s,
    energy_s,
    e_s,
    perm_s,
    local_sem,
    send_sem,
    recv_sem,
):
    nx, nzt, ny, nk = torus
    slabs, cols = nx * nzt, ny * nk
    s = lax.axis_index("slab")
    c = lax.axis_index("col")
    tx, tz = s // nzt, s % nzt
    ty, tk = c // nk, c % nk
    planes_all = slabs * (CX // 2)
    col_low, col_high = jnp.maximum(c - 1, 0), jnp.minimum(c + 1, cols - 1)

    local = [
        pltpu.make_async_copy(ids_hbm.at[c], ids_s.at[0], local_sem.at[0]),
        pltpu.make_async_copy(ids_hbm.at[col_low], ids_s.at[1], local_sem.at[1]),
        pltpu.make_async_copy(ids_hbm.at[col_high], ids_s.at[2], local_sem.at[2]),
        pltpu.make_async_copy(energy_hbm, energy_s, local_sem.at[3]),
        pltpu.make_async_copy(rows_hbm, rows_s, local_sem.at[4]),
        pltpu.make_async_copy(fields_hbm, raw, local_sem.at[5]),
        pltpu.make_async_copy(mask_hbm, mask, local_sem.at[6]),
        pltpu.make_async_copy(coarse_hbm, cb.at[pl.ds(CAP, CAP)], local_sem.at[7]),
    ]
    for copy in local:
        copy.start()

    def halo_peer(ds, dc):
        return ((s + ds + slabs) % slabs, (c + dc + cols) % cols)

    def torus_peer(dx, dy, dz, dk):
        qx = (tx + dx) % nx if dx else tx
        qy = (ty + dy) % ny if dy else ty
        qz = (tz + dz) % nzt if dz else tz
        qk = (tk + dk) % nk if dk else tk
        return (qx * nzt + qz, qy * nk + qk)

    def far(offset):
        return -sum(min(d, n - d) for d, n in zip(offset, (nx, ny, nzt, nk)))

    def offsets(sx, sy, sz, sk):
        every = [
            (a, b, d, e)
            for a in range(sx)
            for b in range(sy)
            for d in range(sz)
            for e in range(sk)
            if (a, b, d, e) != (0, 0, 0, 0)
        ]
        return sorted(every, key=far)

    halo_offsets = [(a, b) for a in (-1, 0, 1) for b in (-1, 0, 1) if (a, b) != (0, 0)]
    group_zk = offsets(1, 1, nzt, nk)
    group_xy = offsets(nx, ny, 1, 1)
    group_k = offsets(1, 1, 1, nk)
    group_xyz = offsets(nx, ny, nzt, 1)
    peers = [halo_peer(*o) for o in halo_offsets]
    peers += [torus_peer(*o) for o in group_zk + group_xy]
    barrier = pltpu.get_barrier_semaphore()
    for peer in peers:
        pl.semaphore_signal(barrier, inc=1, device_id=peer, device_id_type=MESH)

    face_offset = ((-1, 0), (1, 0), (0, -1), (0, 1))
    has_flag = (s > 0, s < slabs - 1, c > 0, c < cols - 1)
    has = [jnp.where(flag, 1.0, 0.0).astype(F32) for flag in has_flag]

    def send(src, dst, peer, sem):
        pltpu.make_async_remote_copy(
            src_ref=src,
            dst_ref=dst,
            send_sem=send_sem.at[sem],
            recv_sem=recv_sem.at[sem],
            device_id=peer,
            device_id_type=MESH,
        ).start()

    sub = lax.broadcasted_iota(I32, (CY, NZ), 0)
    lane = lax.broadcasted_iota(I32, (CY, NZ), 1)
    zero_slab = jnp.zeros((CY, NZ), F32)

    def column(view, start):
        rows = jnp.broadcast_to(view[pl.ds(start, 1), :], (CX, NZ))
        for x in range(1, CX):
            rows = jnp.where(sub == x, view[pl.ds(start + CY * x, 1), :], rows)
        return rows

    for copy in local[:3]:
        copy.wait()
    own = [ids_s[0, q, s] for q in range(Q)]
    group = [jnp.int32(-1)] * Q
    for face, (ds, dc) in enumerate(face_offset):
        sn = jnp.clip(s + ds, 0, slabs - 1)
        which = (0, 0, 1, 2)[face]

        def match(r, found, sn=sn, which=which, face=face):
            other = jnp.where(has_flag[face], ids_s[which, r, sn], -1)
            return tuple(jnp.where(o == other, face, g) for o, g in zip(own, found))

        group = lax.fori_loop(0, Q, match, tuple(group))
    first_free = jnp.where(s == 0, 0, jnp.where(s == slabs - 1, 1, jnp.where(c == 0, 2, 3)))
    last_free = jnp.where(c == 0, 2, 3)
    key = []
    for q in range(Q):
        free_rank = jnp.int32(0)
        for p in range(Q):
            if p != q:
                free_rank += jnp.where((group[p] < 0) & (own[p] < own[q]), 1, 0)
        place = jnp.where(free_rank < G, first_free, last_free)
        key.append(jnp.where(group[q] < 0, place, group[q]) * 65536 + own[q])
    for q in range(Q):
        rank = jnp.int32(0)
        for p in range(Q):
            if p != q:
                rank += jnp.where(key[p] < key[q], 1, 0)
        pos_s[q] = rank
    for p in range(Q):
        slot = jnp.int32(0)
        for q in range(1, Q):
            slot = jnp.where(pos_s[q] == p, q, slot)
        perm_s[p] = slot

    local[5].wait()
    for p in range(Q):
        u_ref[p, 8:72, :] = raw[perm_s[p]]
    for j in range(G):
        yf[0, j] = column(u_ref.at[2 * G + j], 8)
        yf[1, j] = column(u_ref.at[3 * G + j], 15)
    local[6].wait()
    for k in range(2):
        ym[0, 8 * k : 8 * k + 8, :] = column(mask, k)
        ym[1, 8 * k : 8 * k + 8, :] = column(mask, 6 + k)

    pl.semaphore_wait(barrier, len(peers))

    for ds, dc in halo_offsets:
        at = pl.ds((1 - ds) * CAP, CAP)
        if dc == 0:
            send(coarse_hbm, cb.at[at], halo_peer(ds, dc), 0)
        else:
            send(coarse_hbm, (cl if dc > 0 else cr).at[at], halo_peer(ds, dc), 1 if dc > 0 else 2)
    field_src = (
        u_ref.at[pl.ds(0, G), pl.ds(8, 8)],
        u_ref.at[pl.ds(G, G), pl.ds(64, 8)],
        yf.at[0],
        yf.at[1],
    )
    mask_src = (mask.at[pl.ds(0, 16)], mask.at[pl.ds(48, 16)], ym.at[0], ym.at[1])
    for face in range(4):
        send(field_src[face], rf.at[face ^ 1], halo_peer(*face_offset[face]), 3)
    for face in range(4):
        send(mask_src[face], rm.at[face ^ 1], halo_peer(*face_offset[face]), 4)

    for q in range(Q):
        for ref in (u_ref, v_ref):
            ref[q, 0:8, :] = zero_slab
            ref[q, 72:80, :] = zero_slab
    local[3].wait()
    for p in range(Q):
        e_s[p] = energy_s[ids_s[0, perm_s[p], s]]
    e_total = e_s[0]
    for p in range(1, Q):
        e_total += e_s[p]
    local[4].wait()
    start_own = jnp.int32(0)
    for i in range(slabs):
        start_own += jnp.where(i < s, rows_s[i], 0)
    end_own = start_own + rows_s[s]
    start_prev = start_own - rows_s[jnp.maximum(s - 1, 0)]

    def sides(f, low_row, high_row):
        total = jnp.where(sub == 0, low_row, pltpu.roll(f, 1, 0))
        total += jnp.where(sub == CY - 1, high_row, pltpu.roll(f, CY - 1, 0))
        total += jnp.where(lane == 0, 0.0, pltpu.roll(f, 1, 1))
        total += jnp.where(lane == NZ - 1, 0.0, pltpu.roll(f, NZ - 1, 1))
        return total

    def inside(src, squares):
        def body(x, carry):
            r = pl.multiple_of(8 * x, 8)
            total = zero_slab
            for q in range(Q):
                f = src[q, pl.ds(r + 8, 8), :]
                around = src[q, pl.ds(r, 8), :] + src[q, pl.ds(r + 16, 8), :]
                raw[q, pl.ds(r, 8), :] = around + sides(f, 0.0, 0.0)
                if squares:
                    total += f * f
            if squares:
                sq[pl.ds(r, 8), :] = total
            return carry

        lax.fori_loop(0, CX, body, 0)

    def add_faces(halo):
        for j in range(G):
            raw[j, 0:8, :] = raw[j, 0:8, :] + halo(0, j)
            raw[G + j, 56:64, :] = raw[G + j, 56:64, :] + halo(1, j)
            low, high = halo(2, j), halo(3, j)
            for x in range(CX):
                at = slice(8 * x, 8 * x + 8)
                row = jnp.where(sub == 0, low[x : x + 1, :], 0.0)
                raw[2 * G + j, at, :] = raw[2 * G + j, at, :] + row
                row = jnp.where(sub == CY - 1, high[x : x + 1, :], 0.0)
                raw[3 * G + j, at, :] = raw[3 * G + j, at, :] + row

    inside(u_ref, True)

    out_row = lax.broadcasted_iota(I32, (128, 64), 0)
    in_row = lax.broadcasted_iota(I32, (128, 64), 1)
    high = out_row >> 3
    low = out_row & 7
    along = jnp.where(
        out_row < 64,
        high,
        jnp.where(out_row < 80, high - 10, jnp.where(out_row < 96, high - 2, low)),
    )
    across = jnp.where(out_row < 96, low, jnp.where(out_row < 112, high - 14, high - 6))

    def node_weight(fine, node):
        twice = 2 * fine - 1
        lower = twice >> 2
        w = (twice - 4 * lower).astype(F32) * 0.25
        return jnp.where(node == lower + 2, 1.0 - w, jnp.where(node == lower + 3, w, 0.0))

    weight_xy = node_weight(along, in_row >> 3) * node_weight(across, in_row & 7)
    node_z = lax.broadcasted_iota(I32, (NZC, NZ), 0)
    fine_z = lax.broadcasted_iota(I32, (NZC, NZ), 1)
    lower_z = (2 * fine_z - 1) >> 2
    w_z = (2 * fine_z - 1 - 4 * lower_z).astype(F32) * 0.25
    weight_z = jnp.where(node_z == jnp.clip(lower_z, 0, NZC - 1), 1.0 - w_z, 0.0) + jnp.where(
        node_z == jnp.clip(lower_z + 1, 0, NZC - 1), w_z, 0.0
    )

    local[7].wait()
    wait_for(cb.at[pl.ds(0, 2 * CAP)], recv_sem.at[0])
    wait_for(cl, recv_sem.at[1])
    wait_for(cr, recv_sem.at[2])
    for i in range(8):
        plane = jnp.clip(s * (CX // 2) - 2 + i, 0, planes_all - 1)
        flat = jnp.where(
            plane < start_own,
            plane - start_prev,
            jnp.where(plane < end_own, CAP + plane - start_own, 2 * CAP + plane - end_own),
        )
        flat = jnp.clip(flat, 0, 3 * CAP - 1)
        mine = cb[flat]
        left = cl[flat, CYC - 2 : CYC, :]
        right = cr[flat, 0:2, :]
        pb[8 * i : 8 * i + 2, :] = jnp.where(c == 0, mine[0:1], left)
        pb[8 * i + 2 : 8 * i + 6, :] = mine
        pb[8 * i + 6 : 8 * i + 8, :] = jnp.where(c == cols - 1, mine[CYC - 1 : CYC], right)
    profile = jnp.dot(weight_xy, pb[...], precision=EXACT, preferred_element_type=F32)
    profile = jnp.dot(profile, weight_z, precision=EXACT, preferred_element_type=F32)
    scaled = TIME_STEP * jnp.exp(2.0 * (profile - 1.0))
    bf[0:64, :] = scaled[0:64] * mask[...].astype(F32)
    bf[64:128, :] = scaled[64:128]

    wait_for(rf, recv_sem.at[3])
    add_faces(lambda face, j: rf[face, j] * has[face])

    def near_b(face):
        at = 64 + 16 * face + 8 * near(face)
        return bf[at : at + 8, :]

    def react(src, dst, offset, shift, sums):
        def body(x, carry):
            r = pl.multiple_of(8 * x, 8)
            b = bf[pl.ds(r, 8), :]
            if shift is None:
                squares = sq[pl.ds(r, 8), :]
            else:
                m, extra = shift
                mb = m * b
                squares = st[0, pl.ds(r, 8), :] + mb * (16.0 * mb - 2.0 * st[1, pl.ds(r, 8), :])
                base = [extra + m * nbg[g, pl.ds(r, 8), :] for g in range(4)]
            common = 5.0 + 3.0 * squares
            acc = [zero_slab] * 6
            for q in range(Q):
                e = e_s[q]
                f = src[q, pl.ds(r + 8, 8), :]
                if shift is not None:
                    f = f - mb
                force = f * ((common - e) + f * (e - 2.0 * f))
                if sums and shift is None and src is not v_ref and offset is not None:
                    around = raw[q, pl.ds(r, 8), :]
                elif shift is None:
                    low_row = hy[0, q - 2 * G, pl.ds(x, 1), :] if q // G == 2 else 0.0
                    high_row = hy[1, q - 3 * G, pl.ds(x, 1), :] if q // G == 3 else 0.0
                    around = src[q, pl.ds(r, 8), :] + src[q, pl.ds(r + 16, 8), :]
                    around += sides(f, low_row, high_row)
                else:
                    around = raw[q, pl.ds(r, 8), :] - base[q // G]
                force = force - around
                a = f - b * force
                if sums:
                    square = a * a
                    ea = e * a
                    step = (force, a, square, square * a, ea, ea * a)
                    acc = [total + value for total, value in zip(acc, step)]
                elif dst is u_ref:
                    acc[0] += a * a
                dst[q, pl.ds(r + (offset or 8 if dst is not out_ref else 0), 8), :] = a
            if not sums:
                if dst is u_ref:
                    sq[pl.ds(r, 8), :] = acc[0]
                return carry
            force_all, t1, t2, t3, te, te2 = acc
            st[0, pl.ds(r, 8), :] = t2
            st[1, pl.ds(r, 8), :] = t1
            total, k0, k1, k2 = carry
            b2 = b * b
            total += b * force_all
            k0 += b * (t1 * (5.0 + 3.0 * t2) - te + te2 - 2.0 * t3) - t1 * nbi[pl.ds(r, 8), :]
            k1 += b2 * (e_total - 80.0 - 42.0 * t2 - 6.0 * t1 * t1 - 2.0 * te)
            k2 += b2 * b * (138.0 * t1 + e_total)
            return total, k0, k1, k2

        start = (zero_slab,) * 4 if sums else 0
        return lax.fori_loop(0, CX, body, start)

    sum_b = zero_slab
    sum_b4 = zero_slab
    sum_bnb = zero_slab
    for x in range(CX):
        b = bf[8 * x : 8 * x + 8, :]
        around = sides(b, 0.0, 0.0)
        if x > 0:
            around += bf[8 * x - 8 : 8 * x, :]
        if x < CX - 1:
            around += bf[8 * x + 8 : 8 * x + 16, :]
        nbi[8 * x : 8 * x + 8, :] = around
        square = b * b
        sum_b += b
        sum_b4 += square * square
        sum_bnb += 16.0 * b * around

    parts = react(u_ref, v_ref, 8, None, True)

    wait_for(rm, recv_sem.at[4])
    for face in range(4):
        at = 64 + 16 * face
        bf[at : at + 16, :] = bf[at : at + 16, :] * rm[face].astype(F32) * has[face]
    face_b = (bf[0:8, :], bf[56:64, :], column(bf, 0), column(bf, 7))
    for face in range(4):
        sum_bnb += 4.0 * face_b[face] * near_b(face)

    for j in range(G):
        for k in range(2):
            ya[0, j, 8 * k : 8 * k + 8, :] = column(v_ref.at[2 * G + j], 8 + k)
            ya[1, j, 8 * k : 8 * k + 8, :] = column(v_ref.at[3 * G + j], 14 + k)

    lane_1 = lax.broadcasted_iota(I32, (1, 128), 1)

    def put_row(at, parts, faces):
        total, k0, k1, k2 = parts
        for face in range(4):
            layer = faces[face][0]
            for j in range(1, G):
                layer = layer + faces[face][j]
            k0 -= layer * near_b(face)
        row = jnp.zeros((1, 128), F32)
        every = (sum_b, total, k0, k1 + sum_bnb, k2, -736.0 * sum_b4)
        for k, part in enumerate(every):
            value = jnp.sum(jnp.sum(part, axis=0, keepdims=True), axis=1, keepdims=True)
            row += jnp.where(lane_1 == k, value, 0.0)
        ar_src[at] = row

    def spread(at, group, landing, sem):
        for k, offset in enumerate(group):
            send(ar_src.at[at], landing.at[k], torus_peer(*offset), sem)

    def gathered(at, landing, sem):
        wait_for(landing, recv_sem.at[sem])
        return ar_src[at] + jnp.sum(landing[...], axis=0)

    def two_multipliers(row):
        got = [
            jnp.sum(jnp.where(lane_1 == k, row, 0.0), axis=1, keepdims=True) for k in range(6)
        ]
        inverse = -1.0 / (16.0 * got[0])
        m_a = got[1] * inverse
        m_b = (got[2] + m_a * (got[3] + m_a * (got[4] + m_a * got[5]))) * inverse
        return jnp.broadcast_to(m_a, (CY, NZ)), jnp.broadcast_to(m_b, (CY, NZ))

    put_row(
        0,
        parts,
        (
            [v_ref[j, 8:16, :] for j in range(G)],
            [v_ref[G + j, 64:72, :] for j in range(G)],
            [ya[0, j, 0:8, :] for j in range(G)],
            [ya[1, j, 8:16, :] for j in range(G)],
        ),
    )
    spread(0, group_zk, ar_1a, 5)

    for k in range(2):
        ys[0, k] = column(st.at[k], 0)
        ys[1, k] = column(st.at[k], 7)
    deep = (
        v_ref.at[pl.ds(0, G), pl.ds(8, 16)],
        v_ref.at[pl.ds(G, G), pl.ds(56, 16)],
        ya.at[0],
        ya.at[1],
    )
    flat = (st.at[:, pl.ds(0, 8)], st.at[:, pl.ds(56, 8)], ys.at[0], ys.at[1])
    for face in range(4):
        peer = halo_peer(*face_offset[face])
        send(deep[face], ra.at[face ^ 1], peer, 6)
        send(flat[face], rs.at[face ^ 1], peer, 7)
    inside(v_ref, False)
    for x in range(CX):
        at = slice(8 * x, 8 * x + 8)
        here = nbi[at, :]
        nbg[0, at, :] = here + near_b(0) if x == 0 else here
        nbg[1, at, :] = here + near_b(1) if x == CX - 1 else here
        nbg[2, at, :] = here + jnp.where(sub == 0, near_b(2)[x : x + 1, :], 0.0)
        nbg[3, at, :] = here + jnp.where(sub == CY - 1, near_b(3)[x : x + 1, :], 0.0)

    ar_src[1] = gathered(0, ar_1a, 5)
    spread(1, group_xy, ar_1b, 8)

    wait_for(ra, recv_sem.at[6])
    wait_for(rs, recv_sem.at[7])
    for face in range(4):
        here, beyond = 8 * near(face), 8 * (1 - near(face))
        at = 64 + 16 * face
        b = near_b(face)
        nbh[face] = bf[at + beyond : at + beyond + 8, :] + face_b[face] + sides(b, 0.0, 0.0)
        for j in range(G):
            value = ra[face, j, here : here + 8, :] * has[face]
            ah[face, j] = value
            if face == 0:
                inner = v_ref[j, 8:16, :]
            elif face == 1:
                inner = v_ref[G + j, 64:72, :]
            elif face == 2:
                inner = ya[0, j, 0:8, :]
            else:
                inner = ya[1, j, 8:16, :]
            outer = ra[face, j, beyond : beyond + 8, :]
            nh[face, j] = outer + inner + sides(value, 0.0, 0.0)
    add_faces(lambda face, j: ah[face, j])

    m0, m1 = two_multipliers(gathered(1, ar_1b, 8))

    wait_for(rf, send_sem.at[3])
    for face in range(4):
        b = near_b(face)
        mb = m0 * b
        squares = rs[face, 0] + mb * (16.0 * mb - 2.0 * rs[face, 1])
        common = 5.0 + 3.0 * squares
        base = m1 + m0 * nbh[face]
        for j in range(G):
            e = e_s[face * G + j]
            f = ah[face, j] - mb
            force = f * ((common - e) + f * (e - 2.0 * f)) - (nh[face, j] - base)
            value = f - b * force
            if face == 0:
                u_ref[j, 0:8, :] = value
            elif face == 1:
                u_ref[G + j, 72:80, :] = value
            else:
                hy[face - 2, j] = value
    react(v_ref, u_ref, 8, (m0, m1), False)

    wait_for(ra, send_sem.at[6])
    wait_for(rs, send_sem.at[7])
    parts = react(u_ref, v_ref, None, None, True)
    for j in range(G):
        y2[0, j] = column(v_ref.at[2 * G + j], 8)
        y2[1, j] = column(v_ref.at[3 * G + j], 15)
    put_row(
        2,
        parts,
        (
            [v_ref[j, 8:16, :] for j in range(G)],
            [v_ref[G + j, 64:72, :] for j in range(G)],
            [y2[0, j] for j in range(G)],
            [y2[1, j] for j in range(G)],
        ),
    )
    spread(2, group_k, ar_2a, 9)
    ar_src[3] = gathered(2, ar_2a, 9)
    spread(3, group_xyz, ar_2b, 10)
    shallow = (
        v_ref.at[pl.ds(0, G), pl.ds(8, 8)],
        v_ref.at[pl.ds(G, G), pl.ds(64, 8)],
        y2.at[0],
        y2.at[1],
    )
    for face in range(4):
        send(shallow[face], r2.at[face ^ 1], halo_peer(*face_offset[face]), 11)
    inside(v_ref, False)
    wait_for(r2, recv_sem.at[11])
    add_faces(lambda face, j: r2[face, j] * has[face])
    wait_for(cb.at[pl.ds(0, 2 * CAP)], send_sem.at[0])
    wait_for(cl, send_sem.at[1])
    wait_for(cr, send_sem.at[2])
    wait_for(rm, send_sem.at[4])
    wait_for(ar_1a, send_sem.at[5])
    wait_for(ar_1b, send_sem.at[8])
    wait_for(ar_2a, send_sem.at[9])
    wait_for(r2, send_sem.at[11])

    m2, m3 = two_multipliers(gathered(3, ar_2b, 10))
    react(v_ref, out_ref, 0, (m2, m3), False)
    wait_for(ar_2b, send_sem.at[10])


def write_out(pos_s, result, out_hbm, sem):
    copies = []
    for q in range(Q):
        copy = pltpu.make_async_copy(result.at[pos_s[q]], out_hbm.at[q], sem.at[q])
        copy.start()
        copies.append(copy)
    for copy in copies:
        copy.wait()


def per_device(torus, order_params, layer_mask, coarse_temp, coarse_rows, grain_ids, energy):
    any_space = pl.BlockSpec(memory_space=pl.ANY)
    smem = pl.BlockSpec(memory_space=pltpu.SMEM)
    vmem = pl.BlockSpec(memory_space=pltpu.VMEM)
    nx, nzt, ny, nk = torus
    slabs = nx * nzt
    rows = CX * CY

    def row_slots(count):
        return pltpu.VMEM((count, 1, 128), F32)

    result, pos = pl.pallas_call(
        functools.partial(kernel, torus),
        out_shape=(
            pltpu.VMEM((Q, rows, NZ), F32),
            jax.ShapeDtypeStruct((Q,), I32),
        ),
        in_specs=[any_space] * 6,
        out_specs=(vmem, smem),
        scratch_shapes=[
            pltpu.VMEM((Q, rows, NZ), F32),
            pltpu.VMEM((rows, NZ), I32),
            pltpu.VMEM((3 * CAP, CYC, NZC), F32),
            pltpu.VMEM((3 * CAP, CYC, NZC), F32),
            pltpu.VMEM((3 * CAP, CYC, NZC), F32),
            pltpu.VMEM((64, NZC), F32),
            pltpu.VMEM((Q, rows + 16, NZ), F32),
            pltpu.VMEM((Q, rows + 16, NZ), F32),
            pltpu.VMEM((128, NZ), F32),
            pltpu.VMEM((rows, NZ), F32),
            pltpu.VMEM((4, rows, NZ), F32),
            pltpu.VMEM((4, 16, NZ), I32),
            pltpu.VMEM((2, 16, NZ), I32),
            pltpu.VMEM((2, G, 8, NZ), F32),
            pltpu.VMEM((4, G, 8, NZ), F32),
            pltpu.VMEM((2, G, 16, NZ), F32),
            pltpu.VMEM((4, G, 16, NZ), F32),
            pltpu.VMEM((2, rows, NZ), F32),
            pltpu.VMEM((2, 2, 8, NZ), F32),
            pltpu.VMEM((4, 2, 8, NZ), F32),
            pltpu.VMEM((rows, NZ), F32),
            pltpu.VMEM((2, G, 8, NZ), F32),
            pltpu.VMEM((4, G, 8, NZ), F32),
            pltpu.VMEM((4, G, 8, NZ), F32),
            pltpu.VMEM((4, 8, NZ), F32),
            pltpu.VMEM((2, G, 8, NZ), F32),
            pltpu.VMEM((4, G, 8, NZ), F32),
            row_slots(4),
            row_slots(nzt * nk - 1),
            row_slots(nx * ny - 1),
            row_slots(nk - 1),
            row_slots(nx * ny * nzt - 1),
            pltpu.SMEM((slabs,), I32),
            pltpu.SMEM((3, Q, slabs), I32),
            pltpu.SMEM(energy.shape, F32),
            pltpu.SMEM((Q,), F32),
            pltpu.SMEM((Q,), I32),
            pltpu.SemaphoreType.DMA((8,)),
            pltpu.SemaphoreType.DMA((12,)),
            pltpu.SemaphoreType.DMA((12,)),
        ],
        compiler_params=pltpu.CompilerParams(collective_id=0, has_side_effects=True),
    )(
        coarse_rows,
        jnp.transpose(grain_ids, (1, 2, 0)),
        energy,
        order_params.reshape(Q, rows, NZ),
        layer_mask.reshape(rows, NZ),
        coarse_temp,
    )
    out = pl.pallas_call(
        write_out,
        out_shape=jax.ShapeDtypeStruct((Q, rows, NZ), F32),
        in_specs=[smem, vmem],
        out_specs=any_space,
        scratch_shapes=[pltpu.SemaphoreType.DMA((Q,))],
    )(pos, pltpu.with_memory_space_constraint(result, pltpu.VMEM))
    return out.reshape(Q, CX, CY, NZ)


def solution(mesh, torus=(4, 8, 4, 2)):
    placed = (
        P(None, "slab", "col", None),
        P("slab", "col", None),
        P("slab", "col", None),
        P(),
        P(),
        P(),
    )
    return jax.shard_map(
        functools.partial(per_device, torus),
        mesh=mesh,
        in_specs=placed,
        out_specs=P(None, "slab", "col", None),
        check_vma=False,
    )
```

time: 50 us -> 40.7 us (0.81)
  Pallas kernels: 45.9 us -> 40.6 us
  local copies, waits for them, and re-layouts: 3.89 us -> 0 us
    pallas_call x1 -> x2, Pallas kernels: 45.9 us -> 40.6 us  [the longest x1 38.8 us: per_device(): pl.pallas_call(functools.partial(kernel, torus), out_shape=(pltpu.VMEM((Q...]
    unnamed x2 -> x0, local copies, waits for them, and re-layouts: 3.89 us -> none
where the time goes in v2:
time: 40.7 us; the launch traced here: 40.6 us
  Pallas kernels  40.6 us (100%)
    pallas_call x1, Pallas kernels, per_device(): pl.pallas_call(functools.partial(kernel, torus), out_shape=(pltpu.VMEM((Q...  38.8 us
    pallas_call x1, Pallas kernels, per_device(): pl.pallas_call(write_out, out_shape=jax.ShapeDtypeStruct((Q, rows, NZ), F...  1.75 us

profile of v2, /device:TPU:1, one launch (start us, length us, event | category | flops | bytes accessed | tf_op | source)
XLA Modules:
  0.0 40.6 jit_solution(8146853169976813658)
XLA Ops:
  0.0 38.8 %shard_map.64 = (f32[16,64,256]{2,1,0:T(8,128)S(1)}, s32[16]{0:T(128)}) custom-call(s32[32]{0:T(128)} %rows_hbm.1, s32[8,16,32]{2,1,0:T(8,128)} %bitcast.5, f32[2208]{0:T(1024)} %energy_hbm.1, f32[16,64,256]{2,1,0:T(8,128)} %bitcast.4, s32[64,256]{1,0:T(8,128)} %bitcast.6, f32[6,4,128]{2,1,0:T(4,128)} %coarse_hbm.1), custom_call_target="tpu_custom_call" | custom-call | tf_op jit(solution)/shard_map/pallas_call | solution.py:609
  38.8 1.8 %shard_map.65 = f32[16,64,256]{2,1,0:T(8,128)} custom-call(s32[16]{0:T(128)} %get-tuple-element.7.pos_s, f32[16,64,256]{2,1,0:T(8,128)S(1)} %get-tuple-element.8.result), custom_call_target="tpu_custom_call" | custom-call | tf_op jit(solution)/shard_map/pallas_call | solution.py:668

commit v3 on v2

--- a/solution.py
+++ b/solution.py
@@ -39,7 +39,6 @@
     mask_hbm,
     coarse_hbm,
     out_ref,
-    pos_s,
     raw,
     mask,
     cb,
@@ -73,10 +72,13 @@
     ar_2a,
     ar_2b,
     rows_s,
+    ids_v,
     ids_s,
     energy_s,
     e_s,
     perm_s,
+    pos_s,
+    token,
     local_sem,
     send_sem,
     recv_sem,
@@ -91,9 +93,9 @@
     col_low, col_high = jnp.maximum(c - 1, 0), jnp.minimum(c + 1, cols - 1)
 
     local = [
-        pltpu.make_async_copy(ids_hbm.at[c], ids_s.at[0], local_sem.at[0]),
-        pltpu.make_async_copy(ids_hbm.at[col_low], ids_s.at[1], local_sem.at[1]),
-        pltpu.make_async_copy(ids_hbm.at[col_high], ids_s.at[2], local_sem.at[2]),
+        pltpu.make_async_copy(ids_hbm.at[c], ids_v.at[0], local_sem.at[0]),
+        pltpu.make_async_copy(ids_hbm.at[col_low], ids_v.at[1], local_sem.at[1]),
+        pltpu.make_async_copy(ids_hbm.at[col_high], ids_v.at[2], local_sem.at[2]),
         pltpu.make_async_copy(energy_hbm, energy_s, local_sem.at[3]),
         pltpu.make_async_copy(rows_hbm, rows_s, local_sem.at[4]),
         pltpu.make_async_copy(fields_hbm, raw, local_sem.at[5]),
@@ -128,15 +130,20 @@
         return sorted(every, key=far)
 
     halo_offsets = [(a, b) for a in (-1, 0, 1) for b in (-1, 0, 1) if (a, b) != (0, 0)]
-    group_zk = offsets(1, 1, nzt, nk)
     group_xy = offsets(nx, ny, 1, 1)
     group_k = offsets(1, 1, 1, nk)
     group_xyz = offsets(nx, ny, nzt, 1)
+
+    def signal(sem, peer):
+        pl.semaphore_signal(sem, inc=1, device_id=peer, device_id_type=MESH)
+
+    steps = [(1, 0, 0), (nx - 1, 0, 0), (0, 1, 0), (0, ny - 1, 0), (0, 0, 1), (0, 0, nzt - 1)]
     peers = [halo_peer(*o) for o in halo_offsets]
-    peers += [torus_peer(*o) for o in group_zk + group_xy]
+    peers += [torus_peer(*o, 0) for o in steps]
+    peers += [torus_peer(*o, 1) for o in steps[4:]]
     barrier = pltpu.get_barrier_semaphore()
     for peer in peers:
-        pl.semaphore_signal(barrier, inc=1, device_id=peer, device_id_type=MESH)
+        signal(barrier, peer)
 
     face_offset = ((-1, 0), (1, 0), (0, -1), (0, 1))
     has_flag = (s > 0, s < slabs - 1, c > 0, c < cols - 1)
@@ -162,40 +169,49 @@
             rows = jnp.where(sub == x, view[pl.ds(start + CY * x, 1), :], rows)
         return rows
 
+    sub_i = lax.broadcasted_iota(I32, (Q, 4 * Q), 0)
+    lane_i = lax.broadcasted_iota(I32, (Q, 4 * Q), 1)
+    lane_s = lax.broadcasted_iota(I32, (Q, slabs), 1)
+    sub_q = lax.broadcasted_iota(I32, (Q, Q), 0)
+    lane_q = lax.broadcasted_iota(I32, (Q, Q), 1)
+
+    def ids_of(which, at):
+        picked = jnp.where(lane_s == at, ids_v[which], 0)
+        return jnp.sum(picked, axis=1, keepdims=True)
+
+    def as_row(values):
+        return jnp.sum(jnp.where(sub_q == lane_q, values, 0), axis=0, keepdims=True)
+
     for copy in local[:3]:
         copy.wait()
-    own = [ids_s[0, q, s] for q in range(Q)]
-    group = [jnp.int32(-1)] * Q
-    for face, (ds, dc) in enumerate(face_offset):
-        sn = jnp.clip(s + ds, 0, slabs - 1)
-        which = (0, 0, 1, 2)[face]
-
-        def match(r, found, sn=sn, which=which, face=face):
-            other = jnp.where(has_flag[face], ids_s[which, r, sn], -1)
-            return tuple(jnp.where(o == other, face, g) for o, g in zip(own, found))
-
-        group = lax.fori_loop(0, Q, match, tuple(group))
+    own = ids_of(0, s)
+    beside = (
+        jnp.where(has_flag[0], ids_of(0, jnp.maximum(s - 1, 0)), -1),
+        jnp.where(has_flag[1], ids_of(0, jnp.minimum(s + 1, slabs - 1)), -1),
+        jnp.where(has_flag[2], ids_of(1, s), -1),
+        jnp.where(has_flag[3], ids_of(2, s), -1),
+    )
+    face_i = lane_i >> 4
+    every = jnp.where(
+        face_i < 2,
+        jnp.where(face_i == 0, beside[0], beside[1]),
+        jnp.where(face_i == 2, beside[2], beside[3]),
+    )
+    every = jnp.sum(jnp.where((lane_i & 15) == sub_i, every, 0), axis=0, keepdims=True)
+    found = jnp.sum(jnp.where(own == every, face_i + 1, 0), axis=1, keepdims=True)
+    free = jnp.where(found == 0, own, 65535)
+    free_rank = jnp.sum(jnp.where(as_row(free) < own, 1, 0), axis=1, keepdims=True)
     first_free = jnp.where(s == 0, 0, jnp.where(s == slabs - 1, 1, jnp.where(c == 0, 2, 3)))
     last_free = jnp.where(c == 0, 2, 3)
-    key = []
-    for q in range(Q):
-        free_rank = jnp.int32(0)
-        for p in range(Q):
-            if p != q:
-                free_rank += jnp.where((group[p] < 0) & (own[p] < own[q]), 1, 0)
-        place = jnp.where(free_rank < G, first_free, last_free)
-        key.append(jnp.where(group[q] < 0, place, group[q]) * 65536 + own[q])
-    for q in range(Q):
-        rank = jnp.int32(0)
-        for p in range(Q):
-            if p != q:
-                rank += jnp.where(key[p] < key[q], 1, 0)
-        pos_s[q] = rank
+    place = jnp.where(free_rank < G, first_free, last_free)
+    key = jnp.where(found == 0, place, found - 1) * 65536 + own
+    position = jnp.sum(jnp.where(as_row(key) < key, 1, 0), axis=1, keepdims=True)
+    order = jnp.sum(jnp.where(position == lane_q, sub_q, 0), axis=0, keepdims=True)
+    order = jnp.minimum(order, Q - 1)
+    own_row = as_row(own)
+    position_row = as_row(position)
     for p in range(Q):
-        slot = jnp.int32(0)
-        for q in range(1, Q):
-            slot = jnp.where(pos_s[q] == p, q, slot)
-        perm_s[p] = slot
+        perm_s[p] = order[0, p]
 
     local[5].wait()
     for p in range(Q):
@@ -209,6 +225,8 @@
         ym[1, 8 * k : 8 * k + 8, :] = column(mask, 6 + k)
 
     pl.semaphore_wait(barrier, len(peers))
+    for o in steps:
+        signal(token.at[0], torus_peer(*o, 0))
 
     for ds, dc in halo_offsets:
         at = pl.ds((1 - ds) * CAP, CAP)
@@ -232,9 +250,16 @@
         for ref in (u_ref, v_ref):
             ref[q, 0:8, :] = zero_slab
             ref[q, 72:80, :] = zero_slab
+    pl.semaphore_wait(token.at[0], len(steps))
+    twos = [(2, 0, 0), (0, 2, 0), (0, 0, 2), (0, 0, nzt - 2)]
+    for o in twos:
+        signal(token.at[1], torus_peer(*o, 0))
     local[3].wait()
+    for q in range(Q):
+        pos_s[q] = position_row[0, q]
+        ids_s[q] = own_row[0, q]
     for p in range(Q):
-        e_s[p] = energy_s[ids_s[0, perm_s[p], s]]
+        e_s[p] = energy_s[ids_s[perm_s[p]]]
     e_total = e_s[0]
     for p in range(1, Q):
         e_total += e_s[p]
@@ -281,6 +306,9 @@
                 raw[3 * G + j, at, :] = raw[3 * G + j, at, :] + row
 
     inside(u_ref, True)
+    pl.semaphore_wait(token.at[1], len(twos))
+    for o in group_xy:
+        signal(token.at[2], torus_peer(*o))
 
     out_row = lax.broadcasted_iota(I32, (128, 64), 0)
     in_row = lax.broadcasted_iota(I32, (128, 64), 1)
@@ -353,8 +381,9 @@
             common = 5.0 + 3.0 * squares
             acc = [zero_slab] * 6
             for q in range(Q):
-                e = e_s[q]
-                f = src[q, pl.ds(r + 8, 8), :]
+                p = pos_s[q] if dst is out_ref else q
+                e = e_s[p]
+                f = src[p, pl.ds(r + 8, 8), :]
                 if shift is not None:
                     f = f - mb
                 force = f * ((common - e) + f * (e - 2.0 * f))
@@ -365,6 +394,8 @@
                     high_row = hy[1, q - 3 * G, pl.ds(x, 1), :] if q // G == 3 else 0.0
                     around = src[q, pl.ds(r, 8), :] + src[q, pl.ds(r + 16, 8), :]
                     around += sides(f, low_row, high_row)
+                elif dst is out_ref:
+                    around = raw[p, pl.ds(r, 8), :] - (extra + m * nbg[p >> 2, pl.ds(r, 8), :])
                 else:
                     around = raw[q, pl.ds(r, 8), :] - base[q // G]
                 force = force - around
@@ -435,11 +466,13 @@
             for j in range(1, G):
                 layer = layer + faces[face][j]
             k0 -= layer * near_b(face)
-        row = jnp.zeros((1, 128), F32)
         every = (sum_b, total, k0, k1 + sum_bnb, k2, -736.0 * sum_b4)
+        tile = jnp.zeros((8, 128), F32)
         for k, part in enumerate(every):
-            value = jnp.sum(jnp.sum(part, axis=0, keepdims=True), axis=1, keepdims=True)
-            row += jnp.where(lane_1 == k, value, 0.0)
+            half = part[:, :128] + part[:, 128:]
+            tile = jnp.where(sub[:, :128] == k, jnp.sum(half, axis=0, keepdims=True), tile)
+        tile = jnp.where(sub[:, :128] == lane[:, :128], jnp.sum(tile, axis=1, keepdims=True), 0.0)
+        row = jnp.sum(tile, axis=0, keepdims=True)
         ar_src[at] = row
 
     def spread(at, group, landing, sem):
@@ -469,11 +502,14 @@
             [ya[1, j, 8:16, :] for j in range(G)],
         ),
     )
-    spread(0, group_zk, ar_1a, 5)
+    spread(0, group_k, ar_1a, 5)
 
     for k in range(2):
         ys[0, k] = column(st.at[k], 0)
         ys[1, k] = column(st.at[k], 7)
+    pl.semaphore_wait(token.at[2], len(group_xy))
+    ar_src[1] = gathered(0, ar_1a, 5)
+    spread(1, group_xyz, ar_1b, 8)
     deep = (
         v_ref.at[pl.ds(0, G), pl.ds(8, 16)],
         v_ref.at[pl.ds(G, G), pl.ds(56, 16)],
@@ -493,9 +529,6 @@
         nbg[1, at, :] = here + near_b(1) if x == CX - 1 else here
         nbg[2, at, :] = here + jnp.where(sub == 0, near_b(2)[x : x + 1, :], 0.0)
         nbg[3, at, :] = here + jnp.where(sub == CY - 1, near_b(3)[x : x + 1, :], 0.0)
-
-    ar_src[1] = gathered(0, ar_1a, 5)
-    spread(1, group_xy, ar_1b, 8)
 
     wait_for(ra, recv_sem.at[6])
     wait_for(rs, recv_sem.at[7])
@@ -585,19 +618,14 @@
     wait_for(ar_2b, send_sem.at[10])
 
 
-def write_out(pos_s, result, out_hbm, sem):
-    copies = []
-    for q in range(Q):
-        copy = pltpu.make_async_copy(result.at[pos_s[q]], out_hbm.at[q], sem.at[q])
-        copy.start()
-        copies.append(copy)
-    for copy in copies:
-        copy.wait()
+def write_out(result, out_hbm, sem):
+    copy = pltpu.make_async_copy(result, out_hbm, sem.at[0])
+    copy.start()
+    copy.wait()
 
 
 def per_device(torus, order_params, layer_mask, coarse_temp, coarse_rows, grain_ids, energy):
     any_space = pl.BlockSpec(memory_space=pl.ANY)
-    smem = pl.BlockSpec(memory_space=pltpu.SMEM)
     vmem = pl.BlockSpec(memory_space=pltpu.VMEM)
     nx, nzt, ny, nk = torus
     slabs = nx * nzt
@@ -606,14 +634,11 @@
     def row_slots(count):
         return pltpu.VMEM((count, 1, 128), F32)
 
-    result, pos = pl.pallas_call(
+    result = pl.pallas_call(
         functools.partial(kernel, torus),
-        out_shape=(
-            pltpu.VMEM((Q, rows, NZ), F32),
-            jax.ShapeDtypeStruct((Q,), I32),
-        ),
+        out_shape=pltpu.VMEM((Q, rows, NZ), F32),
         in_specs=[any_space] * 6,
-        out_specs=(vmem, smem),
+        out_specs=vmem,
         scratch_shapes=[
             pltpu.VMEM((Q, rows, NZ), F32),
             pltpu.VMEM((rows, NZ), I32),
@@ -643,15 +668,18 @@
             pltpu.VMEM((2, G, 8, NZ), F32),
             pltpu.VMEM((4, G, 8, NZ), F32),
             row_slots(4),
-            row_slots(nzt * nk - 1),
-            row_slots(nx * ny - 1),
+            row_slots(nk - 1),
+            row_slots(nx * ny * nzt - 1),
             row_slots(nk - 1),
             row_slots(nx * ny * nzt - 1),
             pltpu.SMEM((slabs,), I32),
-            pltpu.SMEM((3, Q, slabs), I32),
+            pltpu.VMEM((3, Q, slabs), I32),
+            pltpu.SMEM((Q,), I32),
             pltpu.SMEM(energy.shape, F32),
             pltpu.SMEM((Q,), F32),
             pltpu.SMEM((Q,), I32),
+            pltpu.SMEM((Q,), I32),
+            pltpu.SemaphoreType.REGULAR((3,)),
             pltpu.SemaphoreType.DMA((8,)),
             pltpu.SemaphoreType.DMA((12,)),
             pltpu.SemaphoreType.DMA((12,)),
@@ -668,10 +696,10 @@
     out = pl.pallas_call(
         write_out,
         out_shape=jax.ShapeDtypeStruct((Q, rows, NZ), F32),
-        in_specs=[smem, vmem],
+        in_specs=[vmem],
         out_specs=any_space,
-        scratch_shapes=[pltpu.SemaphoreType.DMA((Q,))],
-    )(pos, pltpu.with_memory_space_constraint(result, pltpu.VMEM))
+        scratch_shapes=[pltpu.SemaphoreType.DMA((1,))],
+    )(pltpu.with_memory_space_constraint(result, pltpu.VMEM))
     return out.reshape(Q, CX, CY, NZ)
 
 

time: 40.7 us -> 36.1 us (0.89)
  Pallas kernels: 40.6 us -> 36 us
    pallas_call x1, Pallas kernels: 38.8 us -> 35 us  [per_device(): pl.pallas_call(functools.partial(kernel, torus), out_shape=pltpu.VMEM((Q,...]
    pallas_call x1, Pallas kernels: 1.75 us -> 0.98 us  [per_device(): pl.pallas_call(write_out, out_shape=jax.ShapeDtypeStruct((Q, rows, NZ), F...]
where the time goes in v3:
time: 36.1 us; the launch traced here: 36 us
  Pallas kernels  36 us (100%)
    pallas_call x1, Pallas kernels, per_device(): pl.pallas_call(functools.partial(kernel, torus), out_shape=pltpu.VMEM((Q,...  35 us
    pallas_call x1, Pallas kernels, per_device(): pl.pallas_call(write_out, out_shape=jax.ShapeDtypeStruct((Q, rows, NZ), F...  0.98 us

profile of v3, /device:TPU:1, one launch (start us, length us, event | category | flops | bytes accessed | tf_op | source)
XLA Modules:
  0.0 36.0 jit_solution(14812104642844499131)
XLA Ops:
  0.0 35.0 %shard_map.64.result = f32[16,64,256]{2,1,0:T(8,128)S(1)} custom-call(s32[32]{0:T(128)} %rows_hbm.1, s32[8,16,32]{2,1,0:T(8,128)} %bitcast.5, f32[2208]{0:T(1024)} %energy_hbm.1, f32[16,64,256]{2,1,0:T(8,128)} %bitcast.4, s32[64,256]{1,0:T(8,128)} %bitcast.6, f32[6,4,128]{2,1,0:T(4,128)} %coarse_hbm.1), custom_call_target="tpu_custom_call" | custom-call | tf_op jit(solution)/shard_map/pallas_call | solution.py:637
  35.0 1.0 %shard_map.65 = f32[16,64,256]{2,1,0:T(8,128)} custom-call(f32[16,64,256]{2,1,0:T(8,128)S(1)} %shard_map.64.result), custom_call_target="tpu_custom_call" | custom-call | tf_op jit(solution)/shard_map/pallas_call | solution.py:696

commit v4 on v3

--- a/solution.py
+++ b/solution.py
@@ -16,10 +16,10 @@
 CYC = 4
 NZC = 128
 TIME_STEP = 0.05
-EXACT = lax.Precision.HIGHEST
 MESH = pl.DeviceIdType.MESH
 F32 = jnp.float32
 I32 = jnp.int32
+BF16 = jnp.bfloat16
 
 
 def near(face):
@@ -38,7 +38,13 @@
     fields_hbm,
     mask_hbm,
     coarse_hbm,
-    out_ref,
+    last_a,
+    last_n,
+    last_b,
+    last_e,
+    last_s,
+    last_w,
+    last_m,
     raw,
     mask,
     cb,
@@ -68,7 +74,6 @@
     r2,
     ar_src,
     ar_1a,
-    ar_1b,
     ar_2a,
     ar_2b,
     rows_s,
@@ -85,17 +90,7 @@
 ):
     nx, nzt, ny, nk = torus
     slabs, cols = nx * nzt, ny * nk
-    s = lax.axis_index("slab")
-    c = lax.axis_index("col")
-    tx, tz = s // nzt, s % nzt
-    ty, tk = c // nk, c % nk
-    planes_all = slabs * (CX // 2)
-    col_low, col_high = jnp.maximum(c - 1, 0), jnp.minimum(c + 1, cols - 1)
-
     local = [
-        pltpu.make_async_copy(ids_hbm.at[c], ids_v.at[0], local_sem.at[0]),
-        pltpu.make_async_copy(ids_hbm.at[col_low], ids_v.at[1], local_sem.at[1]),
-        pltpu.make_async_copy(ids_hbm.at[col_high], ids_v.at[2], local_sem.at[2]),
         pltpu.make_async_copy(energy_hbm, energy_s, local_sem.at[3]),
         pltpu.make_async_copy(rows_hbm, rows_s, local_sem.at[4]),
         pltpu.make_async_copy(fields_hbm, raw, local_sem.at[5]),
@@ -104,6 +99,21 @@
     ]
     for copy in local:
         copy.start()
+    s = lax.axis_index("slab")
+    c = lax.axis_index("col")
+    tx, tz = s // nzt, s % nzt
+    ty, tk = c // nk, c % nk
+    planes_all = slabs * (CX // 2)
+    col_low, col_high = jnp.maximum(c - 1, 0), jnp.minimum(c + 1, cols - 1)
+
+    local_ids = [
+        pltpu.make_async_copy(ids_hbm.at[c], ids_v.at[0], local_sem.at[0]),
+        pltpu.make_async_copy(ids_hbm.at[col_low], ids_v.at[1], local_sem.at[1]),
+        pltpu.make_async_copy(ids_hbm.at[col_high], ids_v.at[2], local_sem.at[2]),
+    ]
+    for copy in local_ids:
+        copy.start()
+    local = local_ids + local
 
     def halo_peer(ds, dc):
         return ((s + ds + slabs) % slabs, (c + dc + cols) % cols)
@@ -132,6 +142,7 @@
     halo_offsets = [(a, b) for a in (-1, 0, 1) for b in (-1, 0, 1) if (a, b) != (0, 0)]
     group_xy = offsets(nx, ny, 1, 1)
     group_k = offsets(1, 1, 1, nk)
+    group_all = offsets(nx, ny, nzt, nk)
     group_xyz = offsets(nx, ny, nzt, 1)
 
     def signal(sem, peer):
@@ -310,8 +321,8 @@
     for o in group_xy:
         signal(token.at[2], torus_peer(*o))
 
-    out_row = lax.broadcasted_iota(I32, (128, 64), 0)
-    in_row = lax.broadcasted_iota(I32, (128, 64), 1)
+    out_row = lax.broadcasted_iota(I32, (128, 192), 0)
+    in_row = lax.broadcasted_iota(I32, (128, 192), 1) & 63
     high = out_row >> 3
     low = out_row & 7
     along = jnp.where(
@@ -328,8 +339,8 @@
         return jnp.where(node == lower + 2, 1.0 - w, jnp.where(node == lower + 3, w, 0.0))
 
     weight_xy = node_weight(along, in_row >> 3) * node_weight(across, in_row & 7)
-    node_z = lax.broadcasted_iota(I32, (NZC, NZ), 0)
-    fine_z = lax.broadcasted_iota(I32, (NZC, NZ), 1)
+    node_z = lax.broadcasted_iota(I32, (3 * NZC, NZ), 0) & (NZC - 1)
+    fine_z = lax.broadcasted_iota(I32, (3 * NZC, NZ), 1)
     lower_z = (2 * fine_z - 1) >> 2
     w_z = (2 * fine_z - 1 - 4 * lower_z).astype(F32) * 0.25
     weight_z = jnp.where(node_z == jnp.clip(lower_z, 0, NZC - 1), 1.0 - w_z, 0.0) + jnp.where(
@@ -354,8 +365,17 @@
         pb[8 * i : 8 * i + 2, :] = jnp.where(c == 0, mine[0:1], left)
         pb[8 * i + 2 : 8 * i + 6, :] = mine
         pb[8 * i + 6 : 8 * i + 8, :] = jnp.where(c == cols - 1, mine[CYC - 1 : CYC], right)
-    profile = jnp.dot(weight_xy, pb[...], precision=EXACT, preferred_element_type=F32)
-    profile = jnp.dot(profile, weight_z, precision=EXACT, preferred_element_type=F32)
+    def three(value, axis):
+        first = value.astype(BF16)
+        rest = value - first.astype(F32)
+        second = rest.astype(BF16)
+        third = (rest - second.astype(F32)).astype(BF16)
+        return jnp.concatenate([first, second, third], axis=axis)
+
+    weight_xy = weight_xy.astype(BF16)
+    weight_z = weight_z.astype(BF16)
+    profile = jnp.dot(weight_xy, three(pb[...], 0), preferred_element_type=F32)
+    profile = jnp.dot(three(profile, 1), weight_z, preferred_element_type=F32)
     scaled = TIME_STEP * jnp.exp(2.0 * (profile - 1.0))
     bf[0:64, :] = scaled[0:64] * mask[...].astype(F32)
     bf[64:128, :] = scaled[64:128]
@@ -367,7 +387,7 @@
         at = 64 + 16 * face + 8 * near(face)
         return bf[at : at + 8, :]
 
-    def react(src, dst, offset, shift, sums):
+    def react(src, dst, ready, shift, sums):
         def body(x, carry):
             r = pl.multiple_of(8 * x, 8)
             b = bf[pl.ds(r, 8), :]
@@ -381,21 +401,18 @@
             common = 5.0 + 3.0 * squares
             acc = [zero_slab] * 6
             for q in range(Q):
-                p = pos_s[q] if dst is out_ref else q
-                e = e_s[p]
-                f = src[p, pl.ds(r + 8, 8), :]
+                e = e_s[q]
+                f = src[q, pl.ds(r + 8, 8), :]
                 if shift is not None:
                     f = f - mb
                 force = f * ((common - e) + f * (e - 2.0 * f))
-                if sums and shift is None and src is not v_ref and offset is not None:
+                if sums and ready:
                     around = raw[q, pl.ds(r, 8), :]
                 elif shift is None:
                     low_row = hy[0, q - 2 * G, pl.ds(x, 1), :] if q // G == 2 else 0.0
                     high_row = hy[1, q - 3 * G, pl.ds(x, 1), :] if q // G == 3 else 0.0
                     around = src[q, pl.ds(r, 8), :] + src[q, pl.ds(r + 16, 8), :]
                     around += sides(f, low_row, high_row)
-                elif dst is out_ref:
-                    around = raw[p, pl.ds(r, 8), :] - (extra + m * nbg[p >> 2, pl.ds(r, 8), :])
                 else:
                     around = raw[q, pl.ds(r, 8), :] - base[q // G]
                 force = force - around
@@ -407,7 +424,7 @@
                     acc = [total + value for total, value in zip(acc, step)]
                 elif dst is u_ref:
                     acc[0] += a * a
-                dst[q, pl.ds(r + (offset or 8 if dst is not out_ref else 0), 8), :] = a
+                dst[q, pl.ds(r + 8, 8), :] = a
             if not sums:
                 if dst is u_ref:
                     sq[pl.ds(r, 8), :] = acc[0]
@@ -442,7 +459,7 @@
         sum_b4 += square * square
         sum_bnb += 16.0 * b * around
 
-    parts = react(u_ref, v_ref, 8, None, True)
+    parts = react(u_ref, v_ref, True, None, True)
 
     wait_for(rm, recv_sem.at[4])
     for face in range(4):
@@ -502,14 +519,12 @@
             [ya[1, j, 8:16, :] for j in range(G)],
         ),
     )
-    spread(0, group_k, ar_1a, 5)
+    pl.semaphore_wait(token.at[2], len(group_xy))
+    spread(0, group_all, ar_1a, 5)
 
     for k in range(2):
         ys[0, k] = column(st.at[k], 0)
         ys[1, k] = column(st.at[k], 7)
-    pl.semaphore_wait(token.at[2], len(group_xy))
-    ar_src[1] = gathered(0, ar_1a, 5)
-    spread(1, group_xyz, ar_1b, 8)
     deep = (
         v_ref.at[pl.ds(0, G), pl.ds(8, 16)],
         v_ref.at[pl.ds(G, G), pl.ds(56, 16)],
@@ -552,7 +567,7 @@
             nh[face, j] = outer + inner + sides(value, 0.0, 0.0)
     add_faces(lambda face, j: ah[face, j])
 
-    m0, m1 = two_multipliers(gathered(1, ar_1b, 8))
+    m0, m1 = two_multipliers(gathered(0, ar_1a, 5))
 
     wait_for(rf, send_sem.at[3])
     for face in range(4):
@@ -572,11 +587,11 @@
                 u_ref[G + j, 72:80, :] = value
             else:
                 hy[face - 2, j] = value
-    react(v_ref, u_ref, 8, (m0, m1), False)
+    react(v_ref, u_ref, True, (m0, m1), False)
 
     wait_for(ra, send_sem.at[6])
     wait_for(rs, send_sem.at[7])
-    parts = react(u_ref, v_ref, None, None, True)
+    parts = react(u_ref, v_ref, False, None, True)
     for j in range(G):
         y2[0, j] = column(v_ref.at[2 * G + j], 8)
         y2[1, j] = column(v_ref.at[3 * G + j], 15)
@@ -609,19 +624,51 @@
     wait_for(cr, send_sem.at[2])
     wait_for(rm, send_sem.at[4])
     wait_for(ar_1a, send_sem.at[5])
-    wait_for(ar_1b, send_sem.at[8])
     wait_for(ar_2a, send_sem.at[9])
     wait_for(r2, send_sem.at[11])
 
+    def hand_over(x, carry):
+        r = pl.multiple_of(8 * x, 8)
+        for q in range(Q):
+            p = pos_s[q]
+            last_a[q, pl.ds(r, 8), :] = v_ref[p, pl.ds(r + 8, 8), :]
+            last_n[q, pl.ds(r, 8), :] = raw[p, pl.ds(r, 8), :]
+            last_b[q, pl.ds(r, 8), :] = nbg[p >> 2, pl.ds(r, 8), :]
+        last_s[0, pl.ds(r, 8), :] = st[0, pl.ds(r, 8), :]
+        last_s[1, pl.ds(r, 8), :] = st[1, pl.ds(r, 8), :]
+        last_w[pl.ds(r, 8), :] = bf[pl.ds(r, 8), :]
+        return carry
+
+    lax.fori_loop(0, CX, hand_over, 0)
+    for q in range(Q):
+        last_e[q] = jnp.full((1, NZ), e_s[pos_s[q]], F32)
+
     m2, m3 = two_multipliers(gathered(3, ar_2b, 10))
-    react(v_ref, out_ref, 0, (m2, m3), False)
+    last_m[0] = m2
+    last_m[1] = m3
     wait_for(ar_2b, send_sem.at[10])
 
 
-def write_out(result, out_hbm, sem):
-    copy = pltpu.make_async_copy(result, out_hbm, sem.at[0])
-    copy.start()
-    copy.wait()
+def last_step(a_ref, n_ref, nb_ref, e_ref, s_ref, w_ref, m_ref, out_hbm, done, sem):
+    m2 = m_ref[0]
+    m3 = m_ref[1]
+    copies = []
+    for x in range(CX):
+        at = slice(8 * x, 8 * x + 8)
+        b = w_ref[at, :]
+        mb = m2 * b
+        common = 5.0 + 3.0 * (s_ref[0, at, :] + mb * (16.0 * mb - 2.0 * s_ref[1, at, :]))
+        for q in range(Q):
+            e = e_ref[q]
+            f = a_ref[q, at, :] - mb
+            around = n_ref[q, at, :] - (m3 + m2 * nb_ref[q, at, :])
+            done[q, at, :] = f - b * (f * ((common - e) + f * (e - 2.0 * f)) - around)
+        rows = pl.ds(8 * x, 8)
+        copy = pltpu.make_async_copy(done.at[:, rows], out_hbm.at[:, rows], sem.at[x])
+        copy.start()
+        copies.append(copy)
+    for copy in copies:
+        copy.wait()
 
 
 def per_device(torus, order_params, layer_mask, coarse_temp, coarse_rows, grain_ids, energy):
@@ -631,14 +678,16 @@
     slabs = nx * nzt
     rows = CX * CY
 
+    handed_shapes = [(Q, rows, NZ)] * 3 + [(Q, 1, NZ), (2, rows, NZ), (rows, NZ), (2, CY, NZ)]
+
     def row_slots(count):
         return pltpu.VMEM((count, 1, 128), F32)
 
-    result = pl.pallas_call(
+    handed = pl.pallas_call(
         functools.partial(kernel, torus),
-        out_shape=pltpu.VMEM((Q, rows, NZ), F32),
+        out_shape=tuple(pltpu.VMEM(shape, F32) for shape in handed_shapes),
         in_specs=[any_space] * 6,
-        out_specs=vmem,
+        out_specs=(vmem,) * 7,
         scratch_shapes=[
             pltpu.VMEM((Q, rows, NZ), F32),
             pltpu.VMEM((rows, NZ), I32),
@@ -668,8 +717,7 @@
             pltpu.VMEM((2, G, 8, NZ), F32),
             pltpu.VMEM((4, G, 8, NZ), F32),
             row_slots(4),
-            row_slots(nk - 1),
-            row_slots(nx * ny * nzt - 1),
+            row_slots(nx * ny * nzt * nk - 1),
             row_slots(nk - 1),
             row_slots(nx * ny * nzt - 1),
             pltpu.SMEM((slabs,), I32),
@@ -694,12 +742,12 @@
         coarse_temp,
     )
     out = pl.pallas_call(
-        write_out,
+        last_step,
         out_shape=jax.ShapeDtypeStruct((Q, rows, NZ), F32),
-        in_specs=[vmem],
+        in_specs=[vmem] * 7,
         out_specs=any_space,
-        scratch_shapes=[pltpu.SemaphoreType.DMA((1,))],
-    )(pltpu.with_memory_space_constraint(result, pltpu.VMEM))
+        scratch_shapes=[pltpu.VMEM((Q, rows, NZ), F32), pltpu.SemaphoreType.DMA((CX,))],
+    )(*(pltpu.with_memory_space_constraint(part, pltpu.VMEM) for part in handed))
     return out.reshape(Q, CX, CY, NZ)
 
 

time: 36.1 us -> 36.7 us (1.017)
  Pallas kernels: 36 us -> 36.6 us
    pallas_call x2, Pallas kernels: 36 us -> 36.6 us  [the longest x1 35.4 us: per_device(): pl.pallas_call(functools.partial(kernel, torus), out_shape=tuple((pltpu.V...]
where the time goes in v4:
time: 36.7 us; the launch traced here: 36.6 us
  Pallas kernels  36.6 us (100%)
    pallas_call x1, Pallas kernels, per_device(): pl.pallas_call(functools.partial(kernel, torus), out_shape=tuple((pltpu.V...  35.4 us
    pallas_call x1, Pallas kernels, per_device(): pl.pallas_call(last_step, out_shape=jax.ShapeDtypeStruct((Q, rows, NZ), F...  1.19 us

profile of v4, /device:TPU:1, one launch (start us, length us, event | category | flops | bytes accessed | tf_op | source)
XLA Modules:
  0.0 36.6 jit_solution(10862879287198074473)
XLA Ops:
  0.0 35.4 %shard_map.64 = (f32[16,64,256]{2,1,0:T(8,128)S(1)}, f32[16,64,256]{2,1,0:T(8,128)S(1)}, f32[16,64,256]{2,1,0:T(8,128)S(1)}, f32[16,1,256]{2,1,0:T(1,128)S(1)}, ...) custom-call(s32[32]{0:T(128)} %rows_hbm.1, s32[8,16,32]{2,1,0:T(8,128)} %bitcast.5, ...), custom_call_target="tpu_custom_call" | custom-call | tf_op jit(solution)/shard_map/pallas_call | solution.py:686
  35.5 1.2 %shard_map.65 = f32[16,64,256]{2,1,0:T(8,128)} custom-call(f32[16,64,256]{2,1,0:T(8,128)S(1)} %get-tuple-element.12.a_ref, f32[16,64,256]{2,1,0:T(8,128)S(1)} %get-tuple-element.13.n_ref, f32[16,64,256]{2,1,0:T(8,128)S(1)} %get-tuple-element.14.nb_ref, f32[16,1,256]{2,1,0:T(1,128)S(1)} %get-tuple-element.15.e_ref, ...), custom_call_target="tpu_custom_call" | custom-call | tf_op jit(solution)/shard_map/pallas_call | solution.py:744

commit v5 on v3

--- a/solution.py
+++ b/solution.py
@@ -16,10 +16,10 @@
 CYC = 4
 NZC = 128
 TIME_STEP = 0.05
-EXACT = lax.Precision.HIGHEST
 MESH = pl.DeviceIdType.MESH
 F32 = jnp.float32
 I32 = jnp.int32
+BF16 = jnp.bfloat16
 
 
 def near(face):
@@ -87,8 +87,9 @@
     slabs, cols = nx * nzt, ny * nk
     s = lax.axis_index("slab")
     c = lax.axis_index("col")
-    tx, tz = s // nzt, s % nzt
-    ty, tk = c // nk, c % nk
+    z_bits, k_bits = nzt.bit_length() - 1, nk.bit_length() - 1
+    tx, tz = s >> z_bits, s & (nzt - 1)
+    ty, tk = c >> k_bits, c & (nk - 1)
     planes_all = slabs * (CX // 2)
     col_low, col_high = jnp.maximum(c - 1, 0), jnp.minimum(c + 1, cols - 1)
 
@@ -102,18 +103,19 @@
         pltpu.make_async_copy(mask_hbm, mask, local_sem.at[6]),
         pltpu.make_async_copy(coarse_hbm, cb.at[pl.ds(CAP, CAP)], local_sem.at[7]),
     ]
-    for copy in local:
-        copy.start()
+    for at in (5, 0, 1, 2):
+        local[at].start()
 
     def halo_peer(ds, dc):
-        return ((s + ds + slabs) % slabs, (c + dc + cols) % cols)
+        return ((s + ds) & (slabs - 1), (c + dc) & (cols - 1))
+
+    slab_part = [((tx + d) & (nx - 1)) << z_bits for d in range(nx)]
+    z_part = [(tz + d) & (nzt - 1) for d in range(nzt)]
+    y_part = [((ty + d) & (ny - 1)) << k_bits for d in range(ny)]
+    k_part = [(tk + d) & (nk - 1) for d in range(nk)]
 
     def torus_peer(dx, dy, dz, dk):
-        qx = (tx + dx) % nx if dx else tx
-        qy = (ty + dy) % ny if dy else ty
-        qz = (tz + dz) % nzt if dz else tz
-        qk = (tk + dk) % nk if dk else tk
-        return (qx * nzt + qz, qy * nk + qk)
+        return (slab_part[dx] + z_part[dz], y_part[dy] + k_part[dk])
 
     def far(offset):
         return -sum(min(d, n - d) for d, n in zip(offset, (nx, ny, nzt, nk)))
@@ -144,6 +146,8 @@
     barrier = pltpu.get_barrier_semaphore()
     for peer in peers:
         signal(barrier, peer)
+    for at in (6, 7, 4, 3):
+        local[at].start()
 
     face_offset = ((-1, 0), (1, 0), (0, -1), (0, 1))
     has_flag = (s > 0, s < slabs - 1, c > 0, c < cols - 1)
@@ -213,36 +217,37 @@
     for p in range(Q):
         perm_s[p] = order[0, p]
 
+    pl.semaphore_wait(barrier, len(peers))
+    for o in steps:
+        signal(token.at[0], torus_peer(*o, 0))
+
+    for ds, dc in halo_offsets:
+        at = pl.ds((1 - ds) * CAP, CAP)
+        if dc == 0:
+            send(coarse_hbm, cb.at[at], halo_peer(ds, dc), 0)
+        else:
+            send(coarse_hbm, (cl if dc > 0 else cr).at[at], halo_peer(ds, dc), 1 if dc > 0 else 2)
     local[5].wait()
     for p in range(Q):
         u_ref[p, 8:72, :] = raw[perm_s[p]]
     for j in range(G):
         yf[0, j] = column(u_ref.at[2 * G + j], 8)
         yf[1, j] = column(u_ref.at[3 * G + j], 15)
-    local[6].wait()
-    for k in range(2):
-        ym[0, 8 * k : 8 * k + 8, :] = column(mask, k)
-        ym[1, 8 * k : 8 * k + 8, :] = column(mask, 6 + k)
-
-    pl.semaphore_wait(barrier, len(peers))
-    for o in steps:
-        signal(token.at[0], torus_peer(*o, 0))
-
-    for ds, dc in halo_offsets:
-        at = pl.ds((1 - ds) * CAP, CAP)
-        if dc == 0:
-            send(coarse_hbm, cb.at[at], halo_peer(ds, dc), 0)
-        else:
-            send(coarse_hbm, (cl if dc > 0 else cr).at[at], halo_peer(ds, dc), 1 if dc > 0 else 2)
+
+
     field_src = (
         u_ref.at[pl.ds(0, G), pl.ds(8, 8)],
         u_ref.at[pl.ds(G, G), pl.ds(64, 8)],
         yf.at[0],
         yf.at[1],
     )
-    mask_src = (mask.at[pl.ds(0, 16)], mask.at[pl.ds(48, 16)], ym.at[0], ym.at[1])
     for face in range(4):
         send(field_src[face], rf.at[face ^ 1], halo_peer(*face_offset[face]), 3)
+    local[6].wait()
+    for k in range(2):
+        ym[0, 8 * k : 8 * k + 8, :] = column(mask, k)
+        ym[1, 8 * k : 8 * k + 8, :] = column(mask, 6 + k)
+    mask_src = (mask.at[pl.ds(0, 16)], mask.at[pl.ds(48, 16)], ym.at[0], ym.at[1])
     for face in range(4):
         send(mask_src[face], rm.at[face ^ 1], halo_peer(*face_offset[face]), 4)
 
@@ -270,12 +275,21 @@
     end_own = start_own + rows_s[s]
     start_prev = start_own - rows_s[jnp.maximum(s - 1, 0)]
 
+    lane_h = lax.broadcasted_iota(I32, (CY, 128), 1)
+
     def sides(f, low_row, high_row):
         total = jnp.where(sub == 0, low_row, pltpu.roll(f, 1, 0))
         total += jnp.where(sub == CY - 1, high_row, pltpu.roll(f, CY - 1, 0))
-        total += jnp.where(lane == 0, 0.0, pltpu.roll(f, 1, 1))
-        total += jnp.where(lane == NZ - 1, 0.0, pltpu.roll(f, NZ - 1, 1))
-        return total
+        left, right = f[:, :128], f[:, 128:]
+        left_up, right_up = pltpu.roll(left, 1, 1), pltpu.roll(right, 1, 1)
+        left_down, right_down = pltpu.roll(left, 127, 1), pltpu.roll(right, 127, 1)
+        first = jnp.where(lane_h == 0, 0.0, left_up) + jnp.where(
+            lane_h == 127, right_down, left_down
+        )
+        second = jnp.where(lane_h == 0, left_up, right_up) + jnp.where(
+            lane_h == 127, 0.0, right_down
+        )
+        return total + jnp.concatenate([first, second], axis=1)
 
     def inside(src, squares):
         def body(x, carry):
@@ -310,8 +324,8 @@
     for o in group_xy:
         signal(token.at[2], torus_peer(*o))
 
-    out_row = lax.broadcasted_iota(I32, (128, 64), 0)
-    in_row = lax.broadcasted_iota(I32, (128, 64), 1)
+    out_row = lax.broadcasted_iota(I32, (128, 192), 0)
+    in_row = lax.broadcasted_iota(I32, (128, 192), 1) & 63
     high = out_row >> 3
     low = out_row & 7
     along = jnp.where(
@@ -328,13 +342,15 @@
         return jnp.where(node == lower + 2, 1.0 - w, jnp.where(node == lower + 3, w, 0.0))
 
     weight_xy = node_weight(along, in_row >> 3) * node_weight(across, in_row & 7)
-    node_z = lax.broadcasted_iota(I32, (NZC, NZ), 0)
-    fine_z = lax.broadcasted_iota(I32, (NZC, NZ), 1)
+    node_z = lax.broadcasted_iota(I32, (3 * NZC, NZ), 0) & (NZC - 1)
+    fine_z = lax.broadcasted_iota(I32, (3 * NZC, NZ), 1)
     lower_z = (2 * fine_z - 1) >> 2
     w_z = (2 * fine_z - 1 - 4 * lower_z).astype(F32) * 0.25
     weight_z = jnp.where(node_z == jnp.clip(lower_z, 0, NZC - 1), 1.0 - w_z, 0.0) + jnp.where(
         node_z == jnp.clip(lower_z + 1, 0, NZC - 1), w_z, 0.0
     )
+    weight_xy = weight_xy.astype(BF16)
+    weight_z = weight_z.astype(BF16)
 
     local[7].wait()
     wait_for(cb.at[pl.ds(0, 2 * CAP)], recv_sem.at[0])
@@ -354,8 +370,15 @@
         pb[8 * i : 8 * i + 2, :] = jnp.where(c == 0, mine[0:1], left)
         pb[8 * i + 2 : 8 * i + 6, :] = mine
         pb[8 * i + 6 : 8 * i + 8, :] = jnp.where(c == cols - 1, mine[CYC - 1 : CYC], right)
-    profile = jnp.dot(weight_xy, pb[...], precision=EXACT, preferred_element_type=F32)
-    profile = jnp.dot(profile, weight_z, precision=EXACT, preferred_element_type=F32)
+    def three(value, axis):
+        first = value.astype(BF16)
+        rest = value - first.astype(F32)
+        second = rest.astype(BF16)
+        third = (rest - second.astype(F32)).astype(BF16)
+        return jnp.concatenate([first, second, third], axis=axis)
+
+    profile = jnp.dot(weight_xy, three(pb[...], 0), preferred_element_type=F32)
+    profile = jnp.dot(three(profile, 1), weight_z, preferred_element_type=F32)
     scaled = TIME_STEP * jnp.exp(2.0 * (profile - 1.0))
     bf[0:64, :] = scaled[0:64] * mask[...].astype(F32)
     bf[64:128, :] = scaled[64:128]
@@ -424,7 +447,7 @@
             return total, k0, k1, k2
 
         start = (zero_slab,) * 4 if sums else 0
-        return lax.fori_loop(0, CX, body, start)
+        return lax.fori_loop(0, CX, body, start, unroll=True)
 
     sum_b = zero_slab
     sum_b4 = zero_slab
@@ -453,9 +476,8 @@
         sum_bnb += 4.0 * face_b[face] * near_b(face)
 
     for j in range(G):
-        for k in range(2):
-            ya[0, j, 8 * k : 8 * k + 8, :] = column(v_ref.at[2 * G + j], 8 + k)
-            ya[1, j, 8 * k : 8 * k + 8, :] = column(v_ref.at[3 * G + j], 14 + k)
+        ya[0, j, 0:8, :] = column(v_ref.at[2 * G + j], 8)
+        ya[1, j, 8:16, :] = column(v_ref.at[3 * G + j], 15)
 
     lane_1 = lax.broadcasted_iota(I32, (1, 128), 1)
 
@@ -504,6 +526,9 @@
     )
     spread(0, group_k, ar_1a, 5)
 
+    for j in range(G):
+        ya[0, j, 8:16, :] = column(v_ref.at[2 * G + j], 9)
+        ya[1, j, 0:8, :] = column(v_ref.at[3 * G + j], 14)
     for k in range(2):
         ys[0, k] = column(st.at[k], 0)
         ys[1, k] = column(st.at[k], 7)

time: 36.1 us -> 35.5 us (0.983)
  Pallas kernels: 36 us -> 35.4 us
    pallas_call x1, Pallas kernels: 35 us -> 34.4 us  [per_device(): pl.pallas_call(functools.partial(kernel, torus), out_shape=pltpu.VMEM((Q,...]
where the time goes in v5:
time: 35.5 us; the launch traced here: 35.4 us
  Pallas kernels  35.4 us (100%)
    pallas_call x1, Pallas kernels, per_device(): pl.pallas_call(functools.partial(kernel, torus), out_shape=pltpu.VMEM((Q,...  34.4 us
    pallas_call x1, Pallas kernels, per_device(): pl.pallas_call(write_out, out_shape=jax.ShapeDtypeStruct((Q, rows, NZ), F...  0.98 us

profile of v5, /device:TPU:1, one launch (start us, length us, event | category | flops | bytes accessed | tf_op | source)
XLA Modules:
  0.0 35.4 jit_solution(11491906663763593538)
XLA Ops:
  0.0 34.4 %shard_map.64.result = f32[16,64,256]{2,1,0:T(8,128)S(1)} custom-call(s32[32]{0:T(128)} %rows_hbm.1, s32[8,16,32]{2,1,0:T(8,128)} %bitcast.5, f32[2208]{0:T(1024)} %energy_hbm.1, f32[16,64,256]{2,1,0:T(8,128)} %bitcast.4, s32[64,256]{1,0:T(8,128)} %bitcast.6, f32[6,4,128]{2,1,0:T(4,128)} %coarse_hbm.1), custom_call_target="tpu_custom_call" | custom-call | tf_op jit(solution)/shard_map/pallas_call | solution.py:662
  34.4 1.0 %shard_map.65 = f32[16,64,256]{2,1,0:T(8,128)} custom-call(f32[16,64,256]{2,1,0:T(8,128)S(1)} %shard_map.64.result), custom_call_target="tpu_custom_call" | custom-call | tf_op jit(solution)/shard_map/pallas_call | solution.py:721

commit v6 on v5

--- a/solution.py
+++ b/solution.py
@@ -38,7 +38,13 @@
     fields_hbm,
     mask_hbm,
     coarse_hbm,
-    out_ref,
+    last_a,
+    last_n,
+    last_b,
+    last_e,
+    last_s,
+    last_w,
+    last_m,
     raw,
     mask,
     cb,
@@ -390,7 +396,7 @@
         at = 64 + 16 * face + 8 * near(face)
         return bf[at : at + 8, :]
 
-    def react(src, dst, offset, shift, sums):
+    def react(src, dst, ready, shift, sums):
         def body(x, carry):
             r = pl.multiple_of(8 * x, 8)
             b = bf[pl.ds(r, 8), :]
@@ -404,21 +410,18 @@
             common = 5.0 + 3.0 * squares
             acc = [zero_slab] * 6
             for q in range(Q):
-                p = pos_s[q] if dst is out_ref else q
-                e = e_s[p]
-                f = src[p, pl.ds(r + 8, 8), :]
+                e = e_s[q]
+                f = src[q, pl.ds(r + 8, 8), :]
                 if shift is not None:
                     f = f - mb
                 force = f * ((common - e) + f * (e - 2.0 * f))
-                if sums and shift is None and src is not v_ref and offset is not None:
+                if sums and ready:
                     around = raw[q, pl.ds(r, 8), :]
                 elif shift is None:
                     low_row = hy[0, q - 2 * G, pl.ds(x, 1), :] if q // G == 2 else 0.0
                     high_row = hy[1, q - 3 * G, pl.ds(x, 1), :] if q // G == 3 else 0.0
                     around = src[q, pl.ds(r, 8), :] + src[q, pl.ds(r + 16, 8), :]
                     around += sides(f, low_row, high_row)
-                elif dst is out_ref:
-                    around = raw[p, pl.ds(r, 8), :] - (extra + m * nbg[p >> 2, pl.ds(r, 8), :])
                 else:
                     around = raw[q, pl.ds(r, 8), :] - base[q // G]
                 force = force - around
@@ -430,7 +433,7 @@
                     acc = [total + value for total, value in zip(acc, step)]
                 elif dst is u_ref:
                     acc[0] += a * a
-                dst[q, pl.ds(r + (offset or 8 if dst is not out_ref else 0), 8), :] = a
+                dst[q, pl.ds(r + 8, 8), :] = a
             if not sums:
                 if dst is u_ref:
                     sq[pl.ds(r, 8), :] = acc[0]
@@ -465,7 +468,7 @@
         sum_b4 += square * square
         sum_bnb += 16.0 * b * around
 
-    parts = react(u_ref, v_ref, 8, None, True)
+    parts = react(u_ref, v_ref, True, None, True)
 
     wait_for(rm, recv_sem.at[4])
     for face in range(4):
@@ -597,11 +600,11 @@
                 u_ref[G + j, 72:80, :] = value
             else:
                 hy[face - 2, j] = value
-    react(v_ref, u_ref, 8, (m0, m1), False)
+    react(v_ref, u_ref, True, (m0, m1), False)
 
     wait_for(ra, send_sem.at[6])
     wait_for(rs, send_sem.at[7])
-    parts = react(u_ref, v_ref, None, None, True)
+    parts = react(u_ref, v_ref, False, None, True)
     for j in range(G):
         y2[0, j] = column(v_ref.at[2 * G + j], 8)
         y2[1, j] = column(v_ref.at[3 * G + j], 15)
@@ -638,15 +641,49 @@
     wait_for(ar_2a, send_sem.at[9])
     wait_for(r2, send_sem.at[11])
 
+    def hand_over(x, carry):
+        r = pl.multiple_of(8 * x, 8)
+        for q in range(Q):
+            p = pos_s[q]
+            last_a[q, pl.ds(r, 8), :] = v_ref[p, pl.ds(r + 8, 8), :]
+            last_n[q, pl.ds(r, 8), :] = raw[p, pl.ds(r, 8), :]
+            last_b[q, pl.ds(r, 8), :] = nbg[p >> 2, pl.ds(r, 8), :]
+        last_s[0, pl.ds(r, 8), :] = st[0, pl.ds(r, 8), :]
+        last_s[1, pl.ds(r, 8), :] = st[1, pl.ds(r, 8), :]
+        last_w[pl.ds(r, 8), :] = bf[pl.ds(r, 8), :]
+        return carry
+
+    lax.fori_loop(0, CX, hand_over, 0)
+    for q in range(Q):
+        last_e[q] = jnp.full((1, NZ), e_s[pos_s[q]], F32)
+
     m2, m3 = two_multipliers(gathered(3, ar_2b, 10))
-    react(v_ref, out_ref, 0, (m2, m3), False)
+    last_m[0] = m2
+    last_m[1] = m3
     wait_for(ar_2b, send_sem.at[10])
 
 
-def write_out(result, out_hbm, sem):
-    copy = pltpu.make_async_copy(result, out_hbm, sem.at[0])
-    copy.start()
-    copy.wait()
+def last_step(a_ref, n_ref, nb_ref, e_ref, s_ref, w_ref, m_ref, out_hbm, done, sem):
+    m2 = m_ref[0]
+    m3 = m_ref[1]
+
+    def body(x, carry):
+        at = pl.ds(pl.multiple_of(8 * x, 8), 8)
+        b = w_ref[at, :]
+        mb = m2 * b
+        common = 5.0 + 3.0 * (s_ref[0, at, :] + mb * (16.0 * mb - 2.0 * s_ref[1, at, :]))
+        for q in range(Q):
+            e = e_ref[q]
+            f = a_ref[q, at, :] - mb
+            around = n_ref[q, at, :] - (m3 + m2 * nb_ref[q, at, :])
+            done[q, at, :] = f - b * (f * ((common - e) + f * (e - 2.0 * f)) - around)
+        pltpu.make_async_copy(done.at[:, at], out_hbm.at[:, at], sem.at[x]).start()
+        return carry
+
+    lax.fori_loop(0, CX, body, 0)
+    for x in range(CX):
+        rows = pl.ds(8 * x, 8)
+        pltpu.make_async_copy(done.at[:, rows], out_hbm.at[:, rows], sem.at[x]).wait()
 
 
 def per_device(torus, order_params, layer_mask, coarse_temp, coarse_rows, grain_ids, energy):
@@ -656,14 +693,16 @@
     slabs = nx * nzt
     rows = CX * CY
 
+    handed_shapes = [(Q, rows, NZ)] * 3 + [(Q, 1, NZ), (2, rows, NZ), (rows, NZ), (2, CY, NZ)]
+
     def row_slots(count):
         return pltpu.VMEM((count, 1, 128), F32)
 
-    result = pl.pallas_call(
+    handed = pl.pallas_call(
         functools.partial(kernel, torus),
-        out_shape=pltpu.VMEM((Q, rows, NZ), F32),
+        out_shape=tuple(pltpu.VMEM(shape, F32) for shape in handed_shapes),
         in_specs=[any_space] * 6,
-        out_specs=vmem,
+        out_specs=(vmem,) * 7,
         scratch_shapes=[
             pltpu.VMEM((Q, rows, NZ), F32),
             pltpu.VMEM((rows, NZ), I32),
@@ -719,12 +758,12 @@
         coarse_temp,
     )
     out = pl.pallas_call(
-        write_out,
+        last_step,
         out_shape=jax.ShapeDtypeStruct((Q, rows, NZ), F32),
-        in_specs=[vmem],
+        in_specs=[vmem] * 7,
         out_specs=any_space,
-        scratch_shapes=[pltpu.SemaphoreType.DMA((1,))],
-    )(pltpu.with_memory_space_constraint(result, pltpu.VMEM))
+        scratch_shapes=[pltpu.VMEM((Q, rows, NZ), F32), pltpu.SemaphoreType.DMA((CX,))],
+    )(*(pltpu.with_memory_space_constraint(part, pltpu.VMEM) for part in handed))
     return out.reshape(Q, CX, CY, NZ)
 
 

time: 35.5 us -> 35.5 us (level)
  no operation moved by 1% of the time
where the time goes in v6:
time: 35.5 us; the launch traced here: 35.4 us
  Pallas kernels  35.4 us (100%)
    pallas_call x1, Pallas kernels, per_device(): pl.pallas_call(functools.partial(kernel, torus), out_shape=tuple((pltpu.V...  34.1 us
    pallas_call x1, Pallas kernels, per_device(): pl.pallas_call(last_step, out_shape=jax.ShapeDtypeStruct((Q, rows, NZ), F...  1.27 us

profile of v6, /device:TPU:1, one launch (start us, length us, event | category | flops | bytes accessed | tf_op | source)
XLA Modules:
  0.0 35.4 jit_solution(4925099391944656653)
XLA Ops:
  0.0 34.1 %shard_map.64 = (f32[16,64,256]{2,1,0:T(8,128)S(1)}, f32[16,64,256]{2,1,0:T(8,128)S(1)}, f32[16,64,256]{2,1,0:T(8,128)S(1)}, f32[16,1,256]{2,1,0:T(1,128)S(1)}, ...) custom-call(s32[32]{0:T(128)} %rows_hbm.1, s32[8,16,32]{2,1,0:T(8,128)} %bitcast.5, ...), custom_call_target="tpu_custom_call" | custom-call | tf_op jit(solution)/shard_map/pallas_call | solution.py:701
  34.2 1.3 %shard_map.65 = f32[16,64,256]{2,1,0:T(8,128)} custom-call(f32[16,64,256]{2,1,0:T(8,128)S(1)} %get-tuple-element.12.a_ref, f32[16,64,256]{2,1,0:T(8,128)S(1)} %get-tuple-element.13.n_ref, f32[16,64,256]{2,1,0:T(8,128)S(1)} %get-tuple-element.14.nb_ref, f32[16,1,256]{2,1,0:T(1,128)S(1)} %get-tuple-element.15.e_ref, ...), custom_call_target="tpu_custom_call" | custom-call | tf_op jit(solution)/shard_map/pallas_call | solution.py:760
